TPU v7x, 512 devices: a whole 4x8x8 slice. The times are simulated.
512 devices in a mesh: tile: 64 (over z, x, y_lo), layer: 8 (over y_hi, core).
Axes of the slice: x: 4, y: 8 (y_hi: 4, y_lo: 2; y = y_hi * 2 + y_lo), z: 8, core: 2. Of those that a mesh axis runs over, the one named last changes fastest.
Arguments:
- screens: float32 [32, 1024, 2048], P('layer', 'tile'), may hold values from -4 to 4
- wind_shift: int32 [32, 2], replicated, may hold values from -16 to 383, as said below
- cone_offset: int32 [6, 32], replicated, may hold values from 0 to 383
- cone_weight: float32 [6, 32], replicated, may hold values from 0.5 to 1.5
- valid_mask: int32 [64, 80], P('tile', 'layer'), may hold values from 0 to 1
- reconstructor: bfloat16 [80, 64, 6, 2, 16384], P('layer', None, None, None, 'tile'), may hold values from -0.0234375 to 0.0234375
Outputs:
- slopes: float32 [64, 6, 2, 80], P('tile', None, None, 'layer')
- commands: float32 [16384], P('tile')
Inputs may be any that keep to these rules, and one draw needn't show every extreme that they name: `wind_shift`: column 0 is a row shift; some layer shifts by 16 and some by -16. Column 1 is a column shift of 0 to 383, and some layer shifts by 384 - 1.
All inputs are finite; a program needn't handle non-finite values.
Results may differ from a plain program's by a relative error of at most 0.0029.
Values may be sent and summed in bfloat16 or wider, within the bound.
A program may use at most 128 MiB of HBM per device.

v0:
```python
import math

import jax
import jax.numpy as jnp
from jax import lax
from jax.sharding import PartitionSpec as P

STARS = 6
NP = 16
NF = 32
SUBCOLS = 80
HALO = 16


def padded_2(cells, sides, width):
    for axis, dim in sides:
        count = lax.axis_size(axis)
        head = lax.slice_in_dim(cells, 0, width, axis=dim)
        tail = lax.slice_in_dim(cells, cells.shape[dim] - width, cells.shape[dim], axis=dim)
        cells = jnp.concatenate(
            [
                lax.ppermute(tail, axis, [(i, (i + 1) % count) for i in range(count)]),
                cells,
                lax.ppermute(head, axis, [((i + 1) % count, i) for i in range(count)]),
            ],
            axis=dim,
        )
    return cells


def left_tables(length, pixels):
    frequency = jnp.arange(length, dtype=jnp.float32) - length // 2
    sample = jnp.arange(pixels, dtype=jnp.float32)
    phase_angle = 2.0 * math.pi * frequency[:, None] * sample[None, :] / length
    return (jnp.cos(phase_angle), -jnp.sin(phase_angle))


def block_tables(span, sub_cols):
    column = jnp.arange(span, dtype=jnp.int32)
    target = jnp.arange(sub_cols * NF, dtype=jnp.int32)
    same_block = column[:, None] // NP == target[None, :] // NF
    sample = (column % NP).astype(jnp.float32)
    frequency = (target % NF).astype(jnp.float32) - NF // 2
    phase_angle = 2.0 * math.pi * sample[:, None] * frequency[None, :] / NF
    block_real = jnp.where(same_block, jnp.cos(phase_angle), 0.0)
    block_imag = jnp.where(same_block, -jnp.sin(phase_angle), 0.0)
    owner = target[:, None] // NF == jnp.arange(sub_cols, dtype=jnp.int32)[None, :]
    ones_table = jnp.where(owner, 1.0, 0.0)
    centred_table = jnp.where(owner, frequency[:, None], 0.0)
    return (block_real, block_imag, ones_table, centred_table)


def dense_centroids(pupil_phase, sub_rows, sub_cols):
    highest = lax.Precision.HIGHEST
    stars_count, pixel_rows, span = pupil_phase.shape
    field = pupil_phase.reshape(stars_count, sub_rows, NP, span)
    field_real = jnp.cos(field)
    field_imag = jnp.sin(field)
    block_real, block_imag, ones_table, centred_table = block_tables(span, sub_cols)
    table_real, table_imag = left_tables(NF, NP)

    def across(values, table):
        return jnp.einsum("grpx,xy->grpy", values, table, precision=highest)

    def down(table, values):
        return jnp.einsum("up,grpy->gruy", table, values, precision=highest)

    section_real = across(field_real, block_real) - across(field_imag, block_imag)
    section_imag = across(field_real, block_imag) + across(field_imag, block_real)
    spot_real = down(table_real, section_real) - down(table_imag, section_imag)
    spot_imag = down(table_real, section_imag) + down(table_imag, section_real)
    intensity = spot_real * spot_real + spot_imag * spot_imag
    centred = jnp.arange(NF, dtype=jnp.float32) - NF // 2
    column_sums = jnp.sum(intensity, axis=2)
    row_moments = jnp.einsum("gruy,u->gry", intensity, centred, precision=highest)
    totals = jnp.einsum("gry,yc->grc", column_sums, ones_table, precision=highest)
    along_cols = jnp.einsum("gry,yc->grc", column_sums, centred_table, precision=highest) / totals
    along_rows = jnp.einsum("gry,yc->grc", row_moments, ones_table, precision=highest) / totals
    return jnp.stack([along_cols, along_rows], axis=2)


def row_window(padded_layer, wind_shift, layer_index, pixel_rows):
    margin = (padded_layer.shape[0] - pixel_rows) // 2
    return lax.dynamic_slice_in_dim(
        padded_layer, margin - wind_shift[layer_index, 0], pixel_rows, 0
    )


def add_footprints(
    running, window, wind_shift, cone_offset, cone_weight, layer_index, first_column, span
):
    updated = []
    for star in range(STARS):
        beginning = first_column + wind_shift[layer_index, 1] + cone_offset[star, layer_index]
        footprint = lax.dynamic_slice_in_dim(window, beginning, span, 1)
        updated.append(running[star] + cone_weight[star, layer_index] * footprint)
    return tuple(updated)


def on_device(screens, wind_shift, cone_offset, cone_weight, valid_mask, reconstructor):
    own_layers, pixel_rows, screen_width = screens.shape
    pupil_width = SUBCOLS * NP
    span = pupil_width // lax.axis_size("layer")
    first_column = lax.axis_index("layer") * span
    everything = lax.all_gather(screens, "layer", axis=0, tiled=True)
    padded = padded_2(everything, (("tile", 1),), HALO)

    def add_layer(layer_index, running):
        layer_slab = lax.dynamic_index_in_dim(padded, layer_index, 0, keepdims=False)
        window = row_window(layer_slab, wind_shift, layer_index, pixel_rows)
        return add_footprints(
            running, window, wind_shift, cone_offset, cone_weight, layer_index, first_column, span
        )

    starting = tuple((jnp.zeros((pixel_rows, span), jnp.float32) for star in range(STARS)))
    pieces = lax.fori_loop(0, padded.shape[0], add_layer, starting)
    pupil_phase = jnp.stack(pieces, axis=0)
    sub_rows = pixel_rows // NP
    sub_cols = span // NP
    slopes = jnp.transpose(dense_centroids(pupil_phase, sub_rows, sub_cols), (1, 0, 2, 3))
    slopes = slopes * valid_mask[:, None, None, :].astype(jnp.float32)
    coarse = slopes.astype(jnp.bfloat16)
    partial_commands = jnp.einsum(
        "jrgac,rgaj->c",
        reconstructor,
        lax.all_gather(coarse, "tile", axis=0, tiled=True),
        preferred_element_type=jnp.float32,
    )
    commands = lax.psum(partial_commands, "layer")
    return (slopes, commands)


def solution(mesh):
    placed = (
        P("layer", "tile", None),
        P(),
        P(),
        P(),
        P("tile", "layer"),
        P("layer", None, None, None, "tile"),
    )
    return jax.shard_map(
        on_device,
        mesh=mesh,
        in_specs=placed,
        out_specs=(P("tile", None, None, "layer"), P("tile")),
        check_vma=False,
    )
```

profile of v0, /device:TPU:1, one launch (start us, length us, event | category | flops | bytes accessed | tf_op | source)
XLA Modules:
  0.0 881.1 jit_solution(6662566896819281923)
XLA Ops:
  7.9 60.7 %all-gather.2.cloned.1.call-done = f32[32,16,2048]{2,1,0:T(8,128)} async-done(((f32[4,16,2048]{2,1,0:T(8,128)}), f32[32,16,2048]{2,1,0:T(8,128)}) %all-gather.2.cloned.1.call-update) | async-done | bytes 4194320 | tf_op jit(solution)/shard_map/all_gather | solution.py:105
  68.6 5.4 collective-permute-start
  74.1 7.5 collective-permute-start.1
  82.3 88.2 %collective-permute-done = f32[32,16,2048]{2,1,0:T(8,128)} collective-permute-done((f32[32,16,2048]{2,1,0:T(8,128)}, f32[32,16,2048]{2,1,0:T(8,128)}, u32[]{:S(2)}, u32[]{:S(2)}) %collective-permute-start) | collective-permute-done | bytes 4194336 | tf_op jit(solution)/shard_map/ppermute | solution.py:22
  170.6 84.3 %collective-permute-done.1 = f32[32,16,2048]{2,1,0:T(8,128)} collective-permute-done((f32[32,16,2048]{2,1,0:T(8,128)}, f32[32,16,2048]{2,1,0:T(8,128)}, u32[]{:S(2)}, u32[]{:S(2)}) %collective-permute-start.1) | collective-permute-done | bytes 4194336 | tf_op jit(solution)/shard_map/ppermute | solution.py:24
  254.9 10.3 %pad_maximum_fusion = f32[32,48,2048]{2,1,0:T(8,128)} fusion(f32[32,16,2048]{2,1,0:T(8,128)} %collective-permute-done.1, f32[32,16,2048]{2,1,0:T(8,128)} %all-gather.2.cloned.1.call-done, f32[32,16,2048]{2,1,0:T(8,128)} %collective-permute-done), kind=kLoop, calls=%fused_computation.20 | loop fusion | flops 6291456 | bytes 25165824 | tf_op jit(solution)/shard_map/concatenate | solution.py:20
  265.2 424.2 %while.27 = (s32[]{:T(128)}, f32[16,160]{1,0:T(8,128)S(1)}, f32[16,160]{1,0:T(8,128)S(1)}, f32[16,160]{1,0:T(8,128)S(1)}, f32[16,160]{1,0:T(8,128)S(1)}, /*index...) while((s32[]{:T(128)}, f32[16,160]{1,0:T(8,128)S(1)}, ...), condition=%wide.region_1.2_spmd.clone, body=%wide.region_0.1_spmd.clone.sunk | while | flops 46120 | bytes 185162 | solution.py:116
  272.2 4.3 bitcast_add_fusion.9
  277.0 1.5 bitcast_add_fusion.8
  285.5 4.3 bitcast_add_fusion.9
  290.3 1.5 bitcast_add_fusion.8
  298.8 4.3 bitcast_add_fusion.9
  303.7 1.5 bitcast_add_fusion.8
  312.1 4.2 bitcast_add_fusion.9
  316.9 1.5 bitcast_add_fusion.8
  325.3 4.2 bitcast_add_fusion.9
  330.1 1.5 bitcast_add_fusion.8
  338.6 4.4 bitcast_add_fusion.9
  343.5 1.5 bitcast_add_fusion.8
  352.0 4.3 bitcast_add_fusion.9
  356.8 1.5 bitcast_add_fusion.8
  365.2 4.2 bitcast_add_fusion.9
  370.0 1.5 bitcast_add_fusion.8
  378.5 4.2 bitcast_add_fusion.9
  383.3 1.5 bitcast_add_fusion.8
  391.7 4.2 bitcast_add_fusion.9
  396.5 1.5 bitcast_add_fusion.8
  404.9 4.2 bitcast_add_fusion.9
  409.8 1.5 bitcast_add_fusion.8
  418.2 4.2 bitcast_add_fusion.9
  423.0 1.5 bitcast_add_fusion.8
  431.4 4.2 bitcast_add_fusion.9
  436.2 1.5 bitcast_add_fusion.8
  444.7 4.2 bitcast_add_fusion.9
  449.5 1.5 bitcast_add_fusion.8
  457.9 4.2 bitcast_add_fusion.9
  462.7 1.5 bitcast_add_fusion.8
  471.1 4.3 bitcast_add_fusion.9
  476.0 1.5 bitcast_add_fusion.8
  484.4 4.3 bitcast_add_fusion.9
  489.3 1.5 bitcast_add_fusion.8
  497.7 4.3 bitcast_add_fusion.9
  511.0 4.2 bitcast_add_fusion.9
  515.8 1.5 bitcast_add_fusion.8
  524.2 4.3 bitcast_add_fusion.9
  537.5 4.2 bitcast_add_fusion.9
  550.7 4.2 bitcast_add_fusion.9
  555.5 1.5 bitcast_add_fusion.8
  564.0 4.2 bitcast_add_fusion.9
  577.2 4.2 bitcast_add_fusion.9
  582.0 1.5 bitcast_add_fusion.8
  590.4 4.2 bitcast_add_fusion.9
  603.7 4.2 bitcast_add_fusion.9
  616.9 4.3 bitcast_add_fusion.9
  630.2 4.3 bitcast_add_fusion.9
  643.5 4.2 bitcast_add_fusion.9
  648.3 1.5 bitcast_add_fusion.8
  656.7 4.2 bitcast_add_fusion.9
  669.9 4.2 bitcast_add_fusion.9
  674.7 1.5 bitcast_add_fusion.8
  683.2 4.2 bitcast_add_fusion.9
  698.7 129.7 %all_gather.7 = bf16[64,6,2,10]{3,2,1,0:T(2,128)(2,1)S(1)} all-gather(bf16[1,6,2,10]{3,2,1,0:T(2,128)(2,1)S(1)} %get-tuple-element.413), channel_id=1, replica_groups=mesh['tile'=64,'layer'=8] {'tile'}, dimensions={0}, use_global_device_ids=true | all-gather | bytes 15600 | tf_op jit(solution)/shard_map/all_gather | solution.py:126
  828.7 2.8 fusion
  831.5 42.8 %psum.7 = f32[256]{0:T(256)} all-reduce(f32[256]{0:T(256)S(1)} %bitcast.132), channel_id=1, replica_groups=mesh['tile'=64,'layer'=8] {'layer'}, use_global_device_ids=true, to_apply=%region_3.4 | all-reduce | flops 256 | bytes 2048 | tf_op jit(solution)/shard_map/psum | solution.py:129
  (148 shorter events, 88.1 us)
Async XLA Ops:
  7.2 61.5 %all-gather.2.cloned.1.call-start = ((), (), s32[]{:S(2)}) async-start(), calls=%async_computation | async-start | bytes 4718592 | tf_op jit(solution)/shard_map/all_gather | solution.py:105
  68.6 102.0 %collective-permute-start = (f32[32,16,2048]{2,1,0:T(8,128)}, f32[32,16,2048]{2,1,0:T(8,128)}, u32[]{:S(2)}, u32[]{:S(2)}) collective-permute-start(f32[32,16,2048]{2,1,0:T(8,128)} %all-gather.2.cloned.1.call-done), channel_id=1, source_target_pairs={{0,8},{8,16},{16,24},{24,32},{32,40},{40,48},{48,56},{56,64},{64,7... | collective-permute-start | bytes 12582920 | tf_op jit(solution)/shard_map/ppermute | solution.py:22
  74.1 180.9 %collective-permute-start.1 = (f32[32,16,2048]{2,1,0:T(8,128)}, f32[32,16,2048]{2,1,0:T(8,128)}, u32[]{:S(2)}, u32[]{:S(2)}) collective-permute-start(f32[32,16,2048]{2,1,0:T(8,128)} %all-gather.2.cloned.1.call-done), channel_id=1, source_target_pairs={{8,0},{16,8},{24,16},{32,24},{40,32},{48,40},{56,48},{64,56},{72,6... | collective-permute-start | bytes 12582920 | tf_op jit(solution)/shard_map/ppermute | solution.py:24
  82.3 182.9 %copy-start = (f32[6,32]{1,0:T(8,128)S(1)}, f32[6,32]{1,0:T(8,128)}, u32[]{:S(2)}) copy-start(f32[6,32]{1,0:T(8,128)} %param.11) | copy-start | bytes 2308
  82.3 182.9 %copy-start.1 = (s32[6,32]{1,0:T(8,128)S(1)}, s32[6,32]{1,0:T(8,128)}, u32[]{:S(2)}) copy-start(s32[6,32]{1,0:T(8,128)} %param.10) | copy-start | bytes 2308
  82.3 182.9 %copy-start.2 = (s32[32,2]{0,1:T(2,128)S(1)}, s32[32,2]{0,1:T(2,128)}, u32[]{:S(2)}) copy-start(s32[32,2]{0,1:T(2,128)} %param.9) | copy-start | bytes 772
Sparse Core Ops, SparseCore 0:
  10.1 58.4 all-gather.1
where the time goes:
time: 890 us; the launch traced here: 881 us
  waiting for transfers between devices  234 us (26%)
  other arithmetic  195 us (22%)
  loops' own time  178 us (20%)
  blocking collectives  172 us (19%)
  local copies, waits for them, and re-layouts  63.3 us (7%)
  between operations  14.3 us (2%)
  starting transfers between devices  12.9 us (1%)
  matrix products  10.9 us (1%)
    add x64, other arithmetic, add_footprints(): updated.append(running[star] + cone_weight[star, layer_index] * footprint)  183 us
    another operation x1, loops' own time, on_device(): pieces = lax.fori_loop(0, padded.shape[0], add_layer, starting)  178 us
    all_gather x1, blocking collectives, on_device(): lax.all_gather(coarse, 'tile', axis=0, tiled=True)  130 us
    ppermute x1, waiting for transfers between devices, padded_2(): lax.ppermute(tail, axis, [(i, (i + 1) % count) for i in range(count)])  88.2 us
    ppermute x1, waiting for transfers between devices, padded_2(): lax.ppermute(head, axis, [((i + 1) % count, i) for i in range(count)])  84.3 us
    all_gather x1, waiting for transfers between devices, on_device(): everything = lax.all_gather(screens, 'layer', axis=0, tiled=True)  60.7 us
    psum x1, blocking collectives, on_device(): commands = lax.psum(partial_commands, 'layer')  42.8 us
    dynamic_slice x32, local copies, waits for them, and re-layouts, add_footprints(): cone_offset[star, layer_index]  21.9 us
  transfers between devices with their start and end apart: 3, of which 3 were waited for; matrix products, arithmetic and copies ran while one was open for 0% of the time, Pallas kernels for 0%

commit v1 on v0

v1 whole, which is shorter than its diff:
```python
import math

import jax
import jax.numpy as jnp
from jax import lax
from jax.experimental import pallas as pl
from jax.experimental.pallas import tpu as pltpu
from jax.sharding import PartitionSpec as P

STARS = 6
NP = 16
SPAN = 160
TILES = 64
UNIT = 2.0 * math.pi / 65536.0
MESH = pl.DeviceIdType.MESH
HIGHEST = lax.Precision.HIGHEST


def modulo_16(q):
    return ((q + 32768) & 65535) - 32768


def filter_tables():
    row = lax.broadcasted_iota(jnp.int32, (128, 128), 0)
    col = lax.broadcasted_iota(jnp.int32, (128, 128), 1)
    gap = row - col
    same = (row >> 4) == (col >> 4)
    sign = jnp.where((gap & 1) == 0, 1.0, -1.0)
    angle = gap.astype(jnp.float32) * (math.pi / 32.0)
    inside = jnp.where(same & (gap != 0), angle, math.pi / 2.0)
    cotangent = jnp.cos(inside) / jnp.sin(inside)
    flips = jnp.where(same, sign, 0.0)
    odd = jnp.where(same & (gap != 0), -16.0 * sign * cotangent, 0.0)
    return flips, odd


def dot(a, b):
    return jnp.dot(a, b, precision=HIGHEST, preferred_element_type=jnp.float32)


def footprint_kernel(wind, cone_offset, cone_weight, screens, coded_ref, rows_3, total):
    layer = lax.axis_index("layer")
    zeros = jnp.zeros((8, 128), jnp.float32)
    for slot in range(4):
        down = (wind[layer * 4 + slot, 0] + 16) % 8
        for m in range(16):
            columns = slice(128 * m, 128 * m + 128)
            band = jnp.concatenate([screens[slot, :, columns], zeros], axis=0)
            rows_3[slot, :, columns] = pltpu.roll(band, down, axis=0)

    lane = lax.broadcasted_iota(jnp.int32, (48, 128), 1)
    lane_24 = lax.broadcasted_iota(jnp.int32, (24, 128), 1)
    tails = [None] * 8
    for star in range(STARS):
        total[star] = jnp.zeros((56, 1280), jnp.float32)
        for slot in range(4):
            which = layer * 4 + slot
            beginning = wind[which, 1] + cone_offset[star, which]
            weight = cone_weight[star, which]
            base = beginning // 128
            turn = beginning % 128
            roll_by = (128 - turn) % 128
            stay = lane_24 < 128 - turn
            group = (wind[which, 0] + 16) // 8
            rows = pl.ds(pl.multiple_of(group * 8, 8), 24)

            def turned(m, slot=slot, base=base, roll_by=roll_by):
                columns = pl.ds(pl.multiple_of((base + m) * 128, 128), 128)
                return pltpu.roll(rows_3[slot, :, columns], roll_by, axis=1)

            before = turned(0)
            for m in range(10):
                after = turned(m + 1)
                columns = slice(128 * m, 128 * m + 128)
                total[star, rows, columns] = total[star, rows, columns] + weight * jnp.where(
                    stay, before, after
                )
                before = after
        code = [
            modulo_16(
                jnp.round(total[star, 0:48, 128 * m : 128 * m + 128] * (1.0 / UNIT)).astype(
                    jnp.int32
                )
            )
            for m in range(10)
        ]
        for block in range(8):
            first, start = (block * SPAN) // 128, (block * SPAN) % 128
            if start == 0:
                main = code[first]
            else:
                main = jnp.where(
                    lane < 128 - start,
                    pltpu.roll(code[first], 128 - start, axis=1),
                    pltpu.roll(code[first + 1], 128 - start, axis=1),
                )
            place = 32 * (star % 4)
            tail = code[first + 1]
            if place != start:
                tail = pltpu.roll(tail, (place - start) % 128, axis=1)
            tail = jnp.where((lane >= place) & (lane < place + 32), tail, 0)
            tails[block] = tail if star % 4 == 0 else tails[block] + tail
            for band in range(3):
                rows = slice(16 * band, 16 * band + 16)
                coded_ref[band, block, pl.ds(16 * star, 16), :] = main[rows].astype(jnp.int16)
                if star in (3, 5):
                    coded_ref[band, block, pl.ds(96 + 16 * (star // 4), 16), :] = tails[block][
                        rows
                    ].astype(jnp.int16)


def footprints(wind_shift, cone_offset, cone_weight, screens):
    return pl.pallas_call(
        footprint_kernel,
        out_shape=jax.ShapeDtypeStruct((3, 8, 128, 128), jnp.int16),
        in_specs=[
            pl.BlockSpec(memory_space=pltpu.SMEM),
            pl.BlockSpec(memory_space=pltpu.SMEM),
            pl.BlockSpec(memory_space=pltpu.SMEM),
            pl.BlockSpec(memory_space=pltpu.VMEM),
        ],
        out_specs=pl.BlockSpec(memory_space=pltpu.VMEM),
        scratch_shapes=[
            pltpu.VMEM((4, 24, 2048), jnp.float32),
            pltpu.VMEM((STARS, 56, 1280), jnp.float32),
        ],
        compiler_params=pltpu.CompilerParams(vmem_limit_bytes=16 * 1024 * 1024),
        name="footprints",
    )(wind_shift, cone_offset, cone_weight, screens)


def front_kernel(
    partial,
    mask_ref,
    slopes_ref,
    all_ref,
    swapped,
    coded,
    landed,
    plane,
    line,
    swap_send,
    swap_recv,
    code_send,
    code_recv,
    plane_send,
    plane_recv,
    line_send,
    line_recv,
):
    tile = lax.axis_index("tile")
    layer = lax.axis_index("layer")
    chip_y = layer // 2
    core = layer % 2
    half = layer // 4
    in_plane = tile % 8
    along = tile // 8

    def at(tile_index, layer_index):
        return (tile_index, layer_index)

    partner = at(tile, layer + 1 - 2 * core)

    def code_target(band, d):
        return at((tile + band - 1 + TILES) % TILES, core * 4 + d)

    def code_source(band, y):
        return at((tile - (band - 1) + TILES) % TILES, y * 2 + half)

    barrier = pltpu.get_barrier_semaphore()

    def greet(where):
        pl.semaphore_signal(barrier, inc=1, device_id=where, device_id_type=MESH)

    greet(partner)
    own_is_target = half == core
    for band in range(3):
        for y in range(4):
            if band == 1:
                @pl.when(jnp.logical_not(own_is_target & (chip_y == y)))
                def _(band=band, y=y):
                    greet(code_source(band, y))
            else:
                greet(code_source(band, y))
    for step in range(1, 8):
        greet(at(along * 8 + (in_plane + step) % 8, layer))
        greet(at(((along + step) % 8) * 8 + in_plane, layer))

    flips, odd = filter_tables()

    pl.semaphore_wait(barrier, 27 - own_is_target.astype(jnp.int32))

    def swap(band):
        return pltpu.make_async_remote_copy(
            src_ref=partial.at[band, pl.ds((1 - core) * 4, 4)],
            dst_ref=swapped.at[band],
            send_sem=swap_send.at[band],
            recv_sem=swap_recv.at[band],
            device_id=partner,
            device_id_type=MESH,
        )

    for band in range(3):
        swap(band).start()

    def code_copy(band, d):
        return pltpu.make_async_remote_copy(
            src_ref=coded.at[band, d],
            dst_ref=landed.at[band, chip_y],
            send_sem=code_send.at[band, d],
            recv_sem=code_recv.at[band, chip_y],
            device_id=code_target(band, d),
            device_id_type=MESH,
        )

    def arrival(band, y):
        return pltpu.make_async_remote_copy(
            src_ref=coded.at[band, 0],
            dst_ref=landed.at[band, y],
            send_sem=code_send.at[band, 0],
            recv_sem=code_recv.at[band, y],
            device_id=code_source(band, y),
            device_id_type=MESH,
        )

    for band in range(3):
        swap(band).wait_recv()
        for d in range(4):
            own = partial[band, core * 4 + d].astype(jnp.int32)
            both = own + swapped[band, d].astype(jnp.int32)
            coded[band, d] = modulo_16(both).astype(jnp.int16)
        for d in range(4):
            if band == 1:
                is_self = core * 4 + d == layer

                @pl.when(jnp.logical_not(is_self))
                def _(band=band, d=d):
                    code_copy(band, d).start()

                @pl.when(is_self)
                def _(band=band, d=d):
                    landed[band, chip_y] = coded[band, d]
            else:
                code_copy(band, d).start()

    for band in range(3):
        for y in range(4):
            if band == 1:
                @pl.when(jnp.logical_not(own_is_target & (chip_y == y)))
                def _(band=band, y=y):
                    arrival(band, y).wait_recv()
            else:
                arrival(band, y).wait_recv()

    phase_code = jnp.zeros((128, 128), jnp.int32)
    for band in range(3):
        for y in range(4):
            phase_code = phase_code + landed[band, y].astype(jnp.int32)
    phase = modulo_16(phase_code).astype(jnp.float32) * UNIT
    field_real = jnp.cos(phase)
    field_imag = jnp.sin(phase)
    along_cols = -16.0 * (
        field_real * dot(field_real, flips) + field_imag * dot(field_imag, flips)
    ) - 2.0 * field_imag * dot(field_real, odd)
    along_rows = -16.0 * (
        field_real * dot(flips, field_real) + field_imag * dot(flips, field_imag)
    ) + 2.0 * field_imag * dot(odd, field_real)

    lane_8 = lax.broadcasted_iota(jnp.int32, (8, 128), 1)
    row_8 = lax.broadcasted_iota(jnp.int32, (8, 128), 0)
    parts = []
    for moment in (along_cols, along_rows):
        blocks = jnp.sum(moment.reshape(8, 16, 128), axis=1)
        shared = jnp.where(row_8 < 4, blocks[6:7, :], blocks[7:8, :])
        shared = jnp.where((lane_8 >> 5) == (row_8 & 3), shared, 0.0)
        parts.append(jnp.concatenate([blocks, shared], axis=1))
    sums = jnp.concatenate(parts, axis=0)
    source = lax.broadcasted_iota(jnp.int32, (256, 128), 0)
    column = lax.broadcasted_iota(jnp.int32, (256, 128), 1) % 10
    wanted = jnp.where(
        source < 128, source >> 4, 8 + ((source >> 4) & 1)
    )
    pick = jnp.where(wanted == column, 1.0 / 8192.0, 0.0)
    pick = jnp.where((source >= 128) & (column < 8), 0.0, pick)
    spread = jnp.where(
        lax.broadcasted_iota(jnp.int32, (10, 128), 0)
        == lax.broadcasted_iota(jnp.int32, (10, 128), 1) % 10,
        1.0,
        0.0,
    )
    lit = dot(mask_ref[...].astype(jnp.float32), spread)
    measured = dot(sums, pick) * lit
    for star in range(STARS):
        for axis in range(2):
            slopes_ref[0, star, axis, :] = measured[axis * 8 + star, 0:10]
    lane_16 = lax.broadcasted_iota(jnp.int32, (16, 128), 1)
    row_16 = lax.broadcasted_iota(jnp.int32, (16, 128), 0)
    entry = (row_16 & 7) * 2 + (row_16 >> 3)
    coarse = measured.astype(jnp.bfloat16).astype(jnp.float32)
    flat = jnp.sum(jnp.where(lane_16 // 10 == entry, coarse, 0.0), axis=0, keepdims=True)
    plane[in_plane] = flat

    def plane_copy(step):
        other = (in_plane + step) % 8
        return pltpu.make_async_remote_copy(
            src_ref=plane.at[in_plane],
            dst_ref=plane.at[in_plane],
            send_sem=plane_send.at[step],
            recv_sem=plane_recv.at[step],
            device_id=at(along * 8 + other, layer),
            device_id_type=MESH,
        )

    def plane_arrival(step):
        other = (in_plane - step + 8) % 8
        return pltpu.make_async_remote_copy(
            src_ref=plane.at[in_plane],
            dst_ref=plane.at[other],
            send_sem=plane_send.at[step],
            recv_sem=plane_recv.at[step],
            device_id=at(along * 8 + other, layer),
            device_id_type=MESH,
        )

    for step in range(1, 8):
        plane_copy(step).start()
    for step in range(1, 8):
        plane_arrival(step).wait_recv()

    def line_copy(step):
        return pltpu.make_async_remote_copy(
            src_ref=plane,
            dst_ref=line.at[along],
            send_sem=line_send.at[step],
            recv_sem=line_recv.at[step],
            device_id=at(((along + step) % 8) * 8 + in_plane, layer),
            device_id_type=MESH,
        )

    def line_arrival(step):
        other = (along - step + 8) % 8
        return pltpu.make_async_remote_copy(
            src_ref=plane,
            dst_ref=line.at[other],
            send_sem=line_send.at[step],
            recv_sem=line_recv.at[step],
            device_id=at(other * 8 + in_plane, layer),
            device_id_type=MESH,
        )

    for step in range(1, 8):
        line_copy(step).start()
    line[along] = plane[...]
    for step in range(1, 8):
        line_arrival(step).wait_recv()
    all_ref[...] = line[...].reshape(TILES, 1, 128)

    for band in range(3):
        swap(band).wait_send()
        for d in range(4):
            if band == 1:
                @pl.when(jnp.logical_not(core * 4 + d == layer))
                def _(band=band, d=d):
                    code_copy(band, d).wait_send()
            else:
                code_copy(band, d).wait_send()
    for step in range(1, 8):
        plane_copy(step).wait_send()
        line_copy(step).wait_send()


def front(partial, valid_mask):
    dma = pltpu.SemaphoreType.DMA
    return pl.pallas_call(
        front_kernel,
        out_shape=(
            jax.ShapeDtypeStruct((1, STARS, 2, 10), jnp.float32),
            jax.ShapeDtypeStruct((TILES, 1, 128), jnp.float32),
        ),
        in_specs=[pl.BlockSpec(memory_space=pltpu.VMEM)] * 2,
        out_specs=(
            pl.BlockSpec(memory_space=pltpu.VMEM),
            pl.BlockSpec(memory_space=pltpu.VMEM),
        ),
        scratch_shapes=[
            pltpu.VMEM((3, 4, 128, 128), jnp.int16),
            pltpu.VMEM((3, 4, 128, 128), jnp.int16),
            pltpu.VMEM((3, 4, 128, 128), jnp.int16),
            pltpu.VMEM((8, 1, 128), jnp.float32),
            pltpu.VMEM((8, 8, 1, 128), jnp.float32),
            dma((3,)),
            dma((3,)),
            dma((3, 4)),
            dma((3, 4)),
            dma((8,)),
            dma((8,)),
            dma((8,)),
            dma((8,)),
        ],
        compiler_params=pltpu.CompilerParams(
            collective_id=0, has_side_effects=True, vmem_limit_bytes=16 * 1024 * 1024
        ),
        name="front",
    )(partial, valid_mask)


def sum_kernel(part_ref, out_ref, rows, send_sem, recv_sem):
    tile = lax.axis_index("tile")
    layer = lax.axis_index("layer")
    barrier = pltpu.get_barrier_semaphore()
    for step in range(1, 8):
        pl.semaphore_signal(
            barrier, inc=1, device_id=(tile, (layer + step) % 8), device_id_type=MESH
        )
    pl.semaphore_wait(barrier, 7)

    def copy(step):
        return pltpu.make_async_remote_copy(
            src_ref=part_ref,
            dst_ref=rows.at[layer],
            send_sem=send_sem.at[step],
            recv_sem=recv_sem.at[step],
            device_id=(tile, (layer + step) % 8),
            device_id_type=MESH,
        )

    def arrival(step):
        other = (layer - step + 8) % 8
        return pltpu.make_async_remote_copy(
            src_ref=part_ref,
            dst_ref=rows.at[other],
            send_sem=send_sem.at[step],
            recv_sem=recv_sem.at[step],
            device_id=(tile, other),
            device_id_type=MESH,
        )

    for step in range(1, 8):
        copy(step).start()
    rows[layer] = part_ref[...]
    for step in range(1, 8):
        arrival(step).wait_recv()
    total = rows[0]
    for k in range(1, 8):
        total = total + rows[k]
    out_ref[...] = total
    for step in range(1, 8):
        copy(step).wait_send()


def sum_over_layers(partial):
    dma = pltpu.SemaphoreType.DMA
    return pl.pallas_call(
        sum_kernel,
        out_shape=jax.ShapeDtypeStruct(partial.shape, jnp.float32),
        in_specs=[pl.BlockSpec(memory_space=pltpu.VMEM)],
        out_specs=pl.BlockSpec(memory_space=pltpu.VMEM),
        scratch_shapes=[
            pltpu.VMEM((8,) + partial.shape, jnp.float32),
            dma((8,)),
            dma((8,)),
        ],
        compiler_params=pltpu.CompilerParams(collective_id=1, has_side_effects=True),
        name="sum_over_layers",
    )(partial)


def on_device(screens, wind_shift, cone_offset, cone_weight, valid_mask, reconstructor):
    partial = footprints(wind_shift, cone_offset, cone_weight, screens)
    slopes, gathered = front(partial, valid_mask)
    coarse = gathered[:, 0, :120].astype(jnp.bfloat16).reshape(TILES, STARS, 2, 10)
    partial = jnp.einsum(
        "jrgac,rgaj->c", reconstructor, coarse, preferred_element_type=jnp.float32
    )
    commands = sum_over_layers(partial.reshape(1, -1)).reshape(-1)
    return slopes, commands


def solution(mesh):
    placed = (
        P("layer", "tile", None),
        P(),
        P(),
        P(),
        P("tile", "layer"),
        P("layer", None, None, None, "tile"),
    )
    return jax.shard_map(
        on_device,
        mesh=mesh,
        in_specs=placed,
        out_specs=(P("tile", None, None, "layer"), P("tile")),
        check_vma=False,
    )
```

time: 890 us -> 60.5 us (0.07)
  waiting for transfers between devices: 234 us -> 0 us
  other arithmetic: 195 us -> 0 us
  loops' own time: 178 us -> 0 us
  blocking collectives: 172 us -> 0 us
  local copies, waits for them, and re-layouts: 63.3 us -> 5.78 us
  Pallas kernels: 0 us -> 49.5 us
  between operations: 14.3 us -> 0.68 us
  starting transfers between devices: 12.9 us -> 0 us
    add x64 -> x0, other arithmetic: 183 us -> none  [add_footprints(): updated.append(running[star] + cone_weight[star, layer_index] * footprint)]
    another operation x1 -> x0, loops' own time: 178 us -> none  [on_device(): pieces = lax.fori_loop(0, padded.shape[0], add_layer, starting)]
    ppermute x2 -> x0, waiting for transfers between devices: 173 us -> none  [the longest x1 88.2 us: padded_2(): lax.ppermute(tail, axis, [(i, (i + 1) % count) for i in range(count)])]
    all_gather x1 -> x0, blocking collectives: 130 us -> none  [on_device(): lax.all_gather(coarse, 'tile', axis=0, tiled=True)]
    dynamic_slice x96 -> x0, local copies, waits for them, and re-layouts: 62.7 us -> none  [the longest x32 21.9 us: add_footprints(): cone_offset[star, layer_index]]
    all_gather x1 -> x0, waiting for transfers between devices: 60.7 us -> none  [on_device(): everything = lax.all_gather(screens, 'layer', axis=0, tiled=True)]
    pallas_call x0 -> x3, Pallas kernels: none -> 49.5 us  [the longest x1 35.8 us: front(): pl.pallas_call(front_kernel, out_shape=(jax.ShapeDtypeStruct((1, STARS, 2...]
    psum x1 -> x0, blocking collectives: 42.8 us -> none  [on_device(): commands = lax.psum(partial_commands, 'layer')]
  transfers between devices with their start and end apart: 3 -> 0, of which waited for: 3 -> 0; matrix products, arithmetic and copies ran while one was open for 0% -> 0% of each run, Pallas kernels for 0% -> 0%
where the time goes in v1:
time: 60.5 us; the launch traced here: 59.3 us
  Pallas kernels  49.5 us (82%)
  local copies, waits for them, and re-layouts  5.78 us (10%)
  matrix products  3.37 us (6%)
  between operations  0.68 us (1%)
    pallas_call x1, Pallas kernels, front(): pl.pallas_call(front_kernel, out_shape=(jax.ShapeDtypeStruct((1, STARS, 2...  35.8 us
    pallas_call x1, Pallas kernels, sum_over_layers(): pl.pallas_call(sum_kernel, out_shape=jax.ShapeDtypeStruct(partial.shape,...  10.6 us
    unnamed x11, local copies, waits for them, and re-layouts  5.62 us
    dot_general x1, matrix products, on_device(): jnp.einsum('jrgac,rgaj->c', reconstructor, coarse, preferred_element_type...  3.37 us
    pallas_call x1, Pallas kernels, footprints(): pl.pallas_call(footprint_kernel, out_shape=jax.ShapeDtypeStruct((3, 8, 12...  3.1 us

profile of v1, /device:TPU:1, one launch (start us, length us, event | category | flops | bytes accessed | tf_op | source)
XLA Modules:
  0.0 59.3 jit_solution(8705977602779411235)
XLA Ops:
  0.6 0.8 %copy.9.wind = s32[32,2]{1,0:T(8,128)S(1)} copy(s32[32,2]{0,1:T(2,128)} %param.7) | data formatting | bytes 512 | tf_op args[1]
  1.4 0.0 copy-start
  1.4 1.0 %copy-done = f32[4,16,2048]{2,1,0:T(8,128)S(1)} copy-done((f32[4,16,2048]{2,1,0:T(8,128)S(1)}, f32[4,16,2048]{2,1,0:T(8,128)}, u32[]{:S(2)}) %copy-start) | copy-done | bytes 524312
  2.4 0.0 copy-start.1
  2.4 0.7 %copy-done.1 = s32[6,32]{1,0:T(8,128)S(1)} copy-done((s32[6,32]{1,0:T(8,128)S(1)}, s32[6,32]{1,0:T(8,128)}, u32[]{:S(2)}) %copy-start.1) | copy-done | bytes 792
  3.1 0.0 copy-start.2
  3.1 0.7 %copy-done.2 = f32[6,32]{1,0:T(8,128)S(1)} copy-done((f32[6,32]{1,0:T(8,128)S(1)}, f32[6,32]{1,0:T(8,128)}, u32[]{:S(2)}) %copy-start.2) | copy-done | bytes 792
  3.8 3.1 %footprints.1.partial = s16[3,8,128,128]{3,2,1,0:T(8,128)(2,1)S(1)} custom-call(s32[32,2]{1,0:T(8,128)S(1)} %copy.9.wind, s32[6,32]{1,0:T(8,128)S(1)} %copy-done.1, f32[6,32]{1,0:T(8,128)S(1)} %copy-done.2, f32[4,16,2048]{2,1,0:T(8,128)S(1)} %copy-done), custom_call_target="tpu_custom_call" | custom-call | tf_op jit(solution)/shard_map/footprints/pallas_call | solution.py:113
  6.9 0.0 copy-start.3
  6.9 0.6 %copy-done.3 = s32[1,10]{1,0:T(1,128)S(1)} copy-done((s32[1,10]{1,0:T(1,128)S(1)}, s32[1,10]{1,0:T(1,128)}, u32[]{:S(2)}) %copy-start.3) | copy-done | bytes 64
  7.6 35.8 %front.1 = (f32[1,6,2,10]{3,2,1,0:T(2,128)S(1)}, f32[64,1,128]{2,1,0:T(1,128)S(1)}) custom-call(s16[3,8,128,128]{3,2,1,0:T(8,128)(2,1)S(1)} %footprints.1.partial, s32[1,10]{1,0:T(1,128)S(1)} %copy-done.3), custom_call_target="tpu_custom_call" | custom-call | tf_op jit(solution)/shard_map/front/pallas_call | solution.py:374
  43.4 0.1 copy.10
  43.6 3.4 %fusion.2.part_ref = f32[1,256]{1,0:T(1,128)} fusion(bf16[10,64,6,2,256]{4,3,2,1,0:T(2,128)(2,1)} %param.11, bf16[64,6,2,10,1]{0,3,2,1,4:T(8,128)(2,1)S(1)} %reshape.15), kind=kOutput, calls=%fused_computation.2 | convolution fusion | flops 3932160 | bytes 3948544 | tf_op jit(solution)/shard_map/jrgac,rgaj->c/dot_general | solution.py:472
  47.0 10.6 %sum_over_layers.1 = f32[1,256]{1,0:T(1,128)} custom-call(f32[1,256]{1,0:T(1,128)} %fusion.2.part_ref), custom_call_target="tpu_custom_call" | custom-call | tf_op jit(solution)/shard_map/sum_over_layers/pallas_call | solution.py:453
  57.5 0.6 %copy.22 = f32[1,6,2,10]{3,2,1,0:T(2,128)} copy(f32[1,6,2,10]{3,2,1,0:T(2,128)S(1)} %get-tuple-element.8) | data formatting | bytes 960
  58.1 1.2 %copy.23 = f32[256]{0:T(256)} copy(f32[256]{0:T(256)} %bitcast.9) | data formatting | bytes 2048
  (2 shorter events, 0.0 us)
Async XLA Ops:
  1.4 1.0 %copy-start = (f32[4,16,2048]{2,1,0:T(8,128)S(1)}, f32[4,16,2048]{2,1,0:T(8,128)}, u32[]{:S(2)}) copy-start(f32[4,16,2048]{2,1,0:T(8,128)} %screens.1) | copy-start | bytes 1572868
  2.4 0.7 %copy-start.1 = (s32[6,32]{1,0:T(8,128)S(1)}, s32[6,32]{1,0:T(8,128)}, u32[]{:S(2)}) copy-start(s32[6,32]{1,0:T(8,128)} %cone_offset.1) | copy-start | bytes 2308
  3.1 0.7 %copy-start.2 = (f32[6,32]{1,0:T(8,128)S(1)}, f32[6,32]{1,0:T(8,128)}, u32[]{:S(2)}) copy-start(f32[6,32]{1,0:T(8,128)} %cone_weight.1) | copy-start | bytes 2308
  6.9 0.7 %copy-start.3 = (s32[1,10]{1,0:T(1,128)S(1)}, s32[1,10]{1,0:T(1,128)}, u32[]{:S(2)}) copy-start(s32[1,10]{1,0:T(1,128)} %mask_ref.1) | copy-start | bytes 124

commit v2 on v0

v2 whole, which is shorter than its diff:
```python
import math

import jax
import jax.numpy as jnp
from jax import lax
from jax.experimental import pallas as pl
from jax.experimental.pallas import tpu as pltpu
from jax.sharding import PartitionSpec as P

STARS = 6
SPAN = 160
TILES = 64
UNIT = 2.0 * math.pi / 65536.0
MESH = pl.DeviceIdType.MESH
F32 = jnp.float32
BF16 = jnp.bfloat16
SINE = (
    1.5707962900208665,
    -0.6459633598429161,
    0.07968848044711395,
    -0.0046722277849454265,
    0.00015082049685476598,
)


def modulo_16(q):
    return ((q + 32768) & 65535) - 32768


def iota(shape, axis):
    return lax.broadcasted_iota(jnp.int32, shape, axis)


def split(x):
    high = x.astype(BF16)
    return high, (x - high.astype(F32)).astype(BF16)


def dot(a, b):
    return jnp.dot(a, b, preferred_element_type=F32)


def sine(q):
    q = jnp.where(q > 16384, 32768 - q, jnp.where(q < -16384, -32768 - q, q))
    x = q.astype(F32) * (1.0 / 16384.0)
    square = x * x
    value = SINE[4]
    for coefficient in SINE[3::-1]:
        value = value * square + coefficient
    return value * x


def filter_tables():
    row = iota((128, 128), 0)
    col = iota((128, 128), 1)
    gap = row - col
    same = (row >> 4) == (col >> 4)
    sign = jnp.where((gap & 1) == 0, 1.0, -1.0)
    angle = gap.astype(F32) * (math.pi / 32.0)
    inside = jnp.where(same & (gap != 0), angle, math.pi / 2.0)
    cotangent = jnp.cos(inside) / jnp.sin(inside)
    flips = jnp.where(same, sign, 0.0)
    odd = jnp.where(same & (gap != 0), -16.0 * sign * cotangent, 0.0)
    return flips, odd


def frame_kernel(
    whole_ref,
    cone_weight,
    lit_ref_in,
    screens_hbm,
    matrix_hbm,
    slopes_ref,
    commands_ref,
    held,
    placed,
    partial,
    swapped,
    coded,
    landed,
    filters,
    low_filter,
    pick_ref,
    lit_ref,
    expand,
    keep,
    plane,
    line,
    matrix,
    own_part,
    parts,
    load_sem,
    swap_send,
    swap_recv,
    code_send,
    code_recv,
    plane_send,
    plane_recv,
    line_send,
    line_recv,
    part_send,
    part_recv,
):
    tile = lax.axis_index("tile")
    layer = lax.axis_index("layer")
    chip_y = layer // 2
    core = layer % 2
    half = layer // 4
    in_plane = tile % 8
    along = tile // 8

    def at(tile_index, layer_index):
        return (tile_index, layer_index)

    partner = at(tile, layer + 1 - 2 * core)

    def code_target(band, d):
        return at((tile + band - 1 + TILES) % TILES, core * 4 + d)

    def code_source(band, y):
        return at((tile - (band - 1) + TILES) % TILES, y * 2 + half)

    def plane_peer(step):
        return at(along * 8 + (in_plane + step + 8) % 8, layer)

    def line_peer(step):
        return at(((along + step + 8) % 8) * 8 + in_plane, layer)

    def layer_peer(step):
        return at(tile, (layer + step + 8) % 8)

    barrier = pltpu.get_barrier_semaphore()

    def greet(where):
        pl.semaphore_signal(barrier, inc=1, device_id=where, device_id_type=MESH)

    greet(partner)
    own_is_target = half == core
    for band in range(3):
        for y in range(4):
            if band == 1:
                @pl.when(jnp.logical_not(own_is_target & (chip_y == y)))
                def _(band=band, y=y):
                    greet(code_source(band, y))
            else:
                greet(code_source(band, y))
    for step in range(1, 8):
        greet(plane_peer(-step))
        greet(line_peer(-step))
        greet(layer_peer(-step))

    screens_load = pltpu.make_async_copy(screens_hbm, held, load_sem.at[0])
    screens_load.start()
    matrix_load = pltpu.make_async_copy(matrix_hbm, matrix, load_sem.at[1])
    matrix_load.start()

    zeros = jnp.zeros((32, 128), F32)
    screens_load.wait()
    for slot in range(4):
        down = whole_ref[0, layer * 4 + slot] + 16
        for m in range(16):
            rows = held[16 * slot : 16 * slot + 16, 128 * m : 128 * m + 128]
            placed[16 * slot + m] = pltpu.roll(
                jnp.concatenate([rows, zeros], axis=0), down, axis=0
            )

    lane = iota((48, 128), 1)

    def add_layers(which_half):
        tails = [None] * 4
        for star in range(STARS):
            total = [None] * 5
            for slot in range(4):
                which = layer * 4 + slot
                beginning = whole_ref[1, which] + whole_ref[2 + star, which]
                weight = cone_weight[star, which]
                first = lax.shift_right_logical(beginning, 7) + 5 * which_half + 16 * slot
                turn = beginning & 127
                roll_by = (128 - turn) & 127
                stay = lane < 128 - turn
                before = pltpu.roll(placed[first], roll_by, axis=1)
                for m in range(5):
                    after = pltpu.roll(placed[first + m + 1], roll_by, axis=1)
                    term = weight * jnp.where(stay, before, after)
                    total[m] = term if slot == 0 else total[m] + term
                    before = after
            code = [
                modulo_16(jnp.round(part * (1.0 / UNIT)).astype(jnp.int32)) for part in total
            ]
            for d in range(4):
                start = 32 * d
                main = code[d]
                if d > 0:
                    main = jnp.where(
                        lane < 128 - start,
                        pltpu.roll(code[d], 128 - start, axis=1),
                        pltpu.roll(code[d + 1], 128 - start, axis=1),
                    )
                place = 32 * (star % 4)
                tail = code[d + 1]
                if place != start:
                    tail = pltpu.roll(tail, (place - start) % 128, axis=1)
                tail = jnp.where((lane >= place) & (lane < place + 32), tail, 0)
                tails[d] = tail if star % 4 == 0 else tails[d] + tail
                for band in range(3):
                    rows = slice(16 * band, 16 * band + 16)
                    block = 4 * which_half + d
                    partial[band, block, 16 * star : 16 * star + 16, :] = main[rows].astype(
                        jnp.int16
                    )
                    if star in (3, 5):
                        at_row = 96 + 16 * (star // 4)
                        partial[band, block, at_row : at_row + 16, :] = tails[d][rows].astype(
                            jnp.int16
                        )

    def remote(source, target, send, recv, where):
        return pltpu.make_async_remote_copy(
            src_ref=source,
            dst_ref=target,
            send_sem=send,
            recv_sem=recv,
            device_id=where,
            device_id_type=MESH,
        )

    def swap(band):
        return remote(
            partial.at[band, pl.ds((1 - core) * 4, 4)],
            swapped.at[band],
            swap_send.at[band],
            swap_recv.at[band],
            partner,
        )

    def code_copy(band, d):
        return remote(
            coded.at[band, d],
            landed.at[band, chip_y],
            code_send.at[band, d],
            code_recv.at[band, chip_y],
            code_target(band, d),
        )

    def code_arrival(band, y):
        return remote(
            coded.at[band, 0],
            landed.at[band, y],
            code_send.at[band, 0],
            code_recv.at[band, y],
            code_source(band, y),
        )

    add_layers(1 - core)
    pl.semaphore_wait(barrier, 34 - own_is_target.astype(jnp.int32))
    for band in range(3):
        swap(band).start()
    add_layers(core)

    for band in range(3):
        swap(band).wait_recv()
        for d in range(4):
            own = partial[band, core * 4 + d].astype(jnp.int32)
            both = own + swapped[band, d].astype(jnp.int32)
            coded[band, d] = modulo_16(both).astype(jnp.int16)
        for d in range(4):
            if band == 1:
                is_self = core * 4 + d == layer

                @pl.when(jnp.logical_not(is_self))
                def _(band=band, d=d):
                    code_copy(band, d).start()

                @pl.when(is_self)
                def _(band=band, d=d):
                    landed[band, chip_y] = coded[band, d]
            else:
                code_copy(band, d).start()

    flips, odd = filter_tables()
    odd_high, odd_low = split(odd)
    filters[0] = flips.astype(BF16)
    filters[1] = odd_high
    low_filter[...] = odd_low
    column = iota((256, 384), 1)
    column = jnp.where(column < 128, column, (column - 128) >> 4)
    source = iota((256, 384), 0)
    wanted = jnp.where(source < 128, source >> 4, 8 + ((source >> 4) & 1))
    pick_ref[...] = jnp.where(wanted == column, 1.0 / 8192.0, 0.0).astype(BF16)
    spread = jnp.where(iota((10, 384), 0) == column[0:10], 1.0, 0.0)
    lit_ref[...] = dot(lit_ref_in[...].astype(F32), spread)
    place = iota((64, 1536), 1)
    begin = 24 * iota((64, 1536), 0)
    expand[...] = jnp.where((place >= begin) & (place < begin + 24), 1.0, 0.0).astype(BF16)
    place = iota((16, 1536), 1)
    entry = ((place >> 2) % 6) * 2 + (place & 1)
    for h in range(2):
        wanted = (entry == iota((16, 1536), 0)) & (((place >> 1) & 1) == h)
        keep[h] = jnp.where(wanted, 1.0, 0.0)

    for band in range(3):
        for y in range(4):
            if band == 1:
                @pl.when(jnp.logical_not(own_is_target & (chip_y == y)))
                def _(band=band, y=y):
                    code_arrival(band, y).wait_recv()
            else:
                code_arrival(band, y).wait_recv()

    code = jnp.zeros((128, 128), jnp.int32)
    for band in range(3):
        for y in range(4):
            code = code + landed[band, y].astype(jnp.int32)
    code = modulo_16(code)
    field_imag = sine(code)
    field_real = sine(modulo_16(code + 16384))
    real_high, real_low = split(field_real)
    imag_high, imag_low = split(field_imag)
    right = jnp.concatenate([filters[0], filters[1]], axis=1)
    across = dot(jnp.concatenate([real_high, real_low, imag_high, imag_low], axis=0), right)
    flipped_real = across[0:128, 0:128] + across[128:256, 0:128]
    flipped_imag = across[256:384, 0:128] + across[384:512, 0:128]
    turned_real = (
        across[0:128, 128:256] + across[128:256, 128:256] + dot(real_high, low_filter[...])
    )
    along_cols = (
        -16.0 * (field_real * flipped_real + field_imag * flipped_imag)
        - 2.0 * field_imag * turned_real
    )
    left = jnp.concatenate([filters[0], filters[1]], axis=0)
    down = dot(left, jnp.concatenate([real_high, real_low, imag_high, imag_low], axis=1))
    flipped_real = down[0:128, 0:128] + down[0:128, 128:256]
    flipped_imag = down[0:128, 256:384] + down[0:128, 384:512]
    turned_real = (
        down[128:256, 0:128] + down[128:256, 128:256] + dot(low_filter[...], real_high)
    )
    along_rows = (
        -16.0 * (field_real * flipped_real + field_imag * flipped_imag)
        + 2.0 * field_imag * turned_real
    )

    lane_8 = iota((8, 128), 1)
    row_8 = iota((8, 128), 0)
    sums = []
    for moment in (along_cols, along_rows):
        blocks = jnp.sum(moment.reshape(8, 16, 128), axis=1)
        shared = jnp.where(row_8 < 4, blocks[6:7, :], blocks[7:8, :])
        shared = jnp.where((lane_8 >> 5) == (row_8 & 3), shared, 0.0)
        sums.append(jnp.concatenate([blocks, shared], axis=1))
    sums = jnp.concatenate(sums, axis=0)
    high, rest = sums.astype(BF16), sums
    rest = rest - high.astype(F32)
    middle, low = split(rest)
    measured = dot(jnp.concatenate([high, middle, low], axis=0), pick_ref[...])
    measured = (measured[0:16] + measured[16:32] + measured[32:48]) * lit_ref[...]
    for star in range(STARS):
        for axis in range(2):
            slopes_ref[0, star, axis, :] = measured[axis * 8 + star, 0:10]
    lane_16 = iota((16, 256), 1)
    row_16 = iota((16, 256), 0)
    entry = (row_16 & 7) * 2 + (row_16 >> 3)
    coarse = measured[:, 128:384].astype(BF16).astype(F32)
    flat = jnp.where(((lane_16 & 15) == entry) & (entry < 12), coarse, 0.0)
    plane[in_plane] = jnp.sum(flat, axis=0, keepdims=True)

    def plane_copy(step):
        return remote(
            plane.at[in_plane],
            plane.at[in_plane],
            plane_send.at[step],
            plane_recv.at[step],
            plane_peer(step),
        )

    def plane_arrival(step):
        other = (in_plane - step + 8) % 8
        return remote(
            plane.at[in_plane],
            plane.at[other],
            plane_send.at[step],
            plane_recv.at[step],
            plane_peer(-step),
        )

    for step in range(1, 8):
        plane_copy(step).start()
    for step in range(1, 8):
        plane_arrival(step).wait_recv()

    def line_copy(step):
        return remote(
            plane, line.at[along], line_send.at[step], line_recv.at[step], line_peer(step)
        )

    def line_arrival(step):
        other = (along - step + 8) % 8
        return remote(
            plane, line.at[other], line_send.at[step], line_recv.at[step], line_peer(-step)
        )

    for step in range(1, 8):
        line_copy(step).start()
    line[along] = plane[...]
    for step in range(1, 8):
        line_arrival(step).wait_recv()

    matrix_load.wait()
    gathered = line[...].reshape(TILES, 256).astype(BF16)
    rows = lax.dot_general(
        gathered[:, 0:160],
        expand[...],
        (((0,), (0,)), ((), ())),
        preferred_element_type=F32,
    )
    total = jnp.zeros((32, 128), F32)
    for j in range(10):
        block = rows[16 * j : 16 * j + 16]
        vector = jnp.concatenate([block * keep[0], block * keep[1]], axis=0).astype(BF16)
        total = total + dot(vector, matrix[1536 * j : 1536 * j + 1536, :])
    own_part[...] = jnp.concatenate(
        [
            jnp.sum(total[0:16], axis=0, keepdims=True),
            jnp.sum(total[16:32], axis=0, keepdims=True),
        ],
        axis=1,
    )

    def part_copy(step):
        return remote(
            own_part, parts.at[layer], part_send.at[step], part_recv.at[step], layer_peer(step)
        )

    def part_arrival(step):
        other = (layer - step + 8) % 8
        return remote(
            own_part, parts.at[other], part_send.at[step], part_recv.at[step], layer_peer(-step)
        )

    for step in range(1, 8):
        part_copy(step).start()
    parts[layer] = own_part[...]
    for step in range(1, 8):
        part_arrival(step).wait_recv()
    total = parts[0]
    for k in range(1, 8):
        total = total + parts[k]
    commands_ref[...] = total

    for band in range(3):
        swap(band).wait_send()
        for d in range(4):
            if band == 1:
                @pl.when(jnp.logical_not(core * 4 + d == layer))
                def _(band=band, d=d):
                    code_copy(band, d).wait_send()
            else:
                code_copy(band, d).wait_send()
    for step in range(1, 8):
        plane_copy(step).wait_send()
        line_copy(step).wait_send()
        part_copy(step).wait_send()


def on_device(screens, wind_shift, cone_offset, cone_weight, valid_mask, reconstructor):
    dma = pltpu.SemaphoreType.DMA
    matrix = reconstructor.reshape(3840, 2, 2, 128).transpose(0, 2, 1, 3).reshape(15360, 128)
    slopes, commands = pl.pallas_call(
        frame_kernel,
        out_shape=(
            jax.ShapeDtypeStruct((1, STARS, 2, 10), F32),
            jax.ShapeDtypeStruct((1, 256), F32),
        ),
        in_specs=[
            pl.BlockSpec(memory_space=pltpu.SMEM),
            pl.BlockSpec(memory_space=pltpu.SMEM),
            pl.BlockSpec(memory_space=pltpu.VMEM),
            pl.BlockSpec(memory_space=pltpu.HBM),
            pl.BlockSpec(memory_space=pltpu.HBM),
        ],
        out_specs=[pl.BlockSpec(memory_space=pltpu.VMEM)] * 2,
        scratch_shapes=[
            pltpu.VMEM((64, 2048), F32),
            pltpu.VMEM((64, 48, 128), F32),
            pltpu.VMEM((3, 8, 128, 128), jnp.int16),
            pltpu.VMEM((3, 4, 128, 128), jnp.int16),
            pltpu.VMEM((3, 4, 128, 128), jnp.int16),
            pltpu.VMEM((3, 4, 128, 128), jnp.int16),
            pltpu.VMEM((2, 128, 128), BF16),
            pltpu.VMEM((128, 128), BF16),
            pltpu.VMEM((256, 384), BF16),
            pltpu.VMEM((1, 384), F32),
            pltpu.VMEM((64, 1536), BF16),
            pltpu.VMEM((2, 16, 1536), F32),
            pltpu.VMEM((8, 1, 256), F32),
            pltpu.VMEM((8, 8, 1, 256), F32),
            pltpu.VMEM((15360, 128), BF16),
            pltpu.VMEM((1, 256), F32),
            pltpu.VMEM((8, 1, 256), F32),
            dma((2,)),
            dma((3,)),
            dma((3,)),
            dma((3, 4)),
            dma((3, 4)),
            dma((8,)),
            dma((8,)),
            dma((8,)),
            dma((8,)),
            dma((8,)),
            dma((8,)),
        ],
        compiler_params=pltpu.CompilerParams(
            collective_id=0, has_side_effects=True, vmem_limit_bytes=66_900_000
        ),
        name="frame",
    )(
        jnp.concatenate([wind_shift.T, cone_offset], axis=0),
        cone_weight,
        valid_mask,
        screens.reshape(64, 2048),
        matrix,
    )
    return slopes, commands.reshape(-1)


def solution(mesh):
    placed = (
        P("layer", "tile", None),
        P(),
        P(),
        P(),
        P("tile", "layer"),
        P("layer", None, None, None, "tile"),
    )
    return jax.shard_map(
        on_device,
        mesh=mesh,
        in_specs=placed,
        out_specs=(P("tile", None, None, "layer"), P("tile")),
        check_vma=False,
    )
```

time: 890 us -> 49.7 us (0.06)
  waiting for transfers between devices: 234 us -> 0 us
  other arithmetic: 195 us -> 1.3 us
  loops' own time: 178 us -> 0 us
  blocking collectives: 172 us -> 0 us
  local copies, waits for them, and re-layouts: 63.3 us -> 2.5 us
  Pallas kernels: 0 us -> 44.5 us
  between operations: 14.3 us -> 0.64 us
  starting transfers between devices: 12.9 us -> 0 us
  matrix products: 10.9 us -> 0 us
    add x64 -> x0, other arithmetic: 183 us -> none  [add_footprints(): updated.append(running[star] + cone_weight[star, layer_index] * footprint)]
    another operation x1 -> x0, loops' own time: 178 us -> none  [on_device(): pieces = lax.fori_loop(0, padded.shape[0], add_layer, starting)]
    ppermute x2 -> x0, waiting for transfers between devices: 173 us -> none  [the longest x1 88.2 us: padded_2(): lax.ppermute(tail, axis, [(i, (i + 1) % count) for i in range(count)])]
    all_gather x1 -> x0, blocking collectives: 130 us -> none  [on_device(): lax.all_gather(coarse, 'tile', axis=0, tiled=True)]
    dynamic_slice x96 -> x0, local copies, waits for them, and re-layouts: 62.7 us -> none  [the longest x32 21.9 us: add_footprints(): cone_offset[star, layer_index]]
    all_gather x1 -> x0, waiting for transfers between devices: 60.7 us -> none  [on_device(): everything = lax.all_gather(screens, 'layer', axis=0, tiled=True)]
    pallas_call x0 -> x1, Pallas kernels: none -> 44.5 us  [on_device(): pl.pallas_call(frame_kernel, out_shape=(jax.ShapeDtypeStruct((1, STARS, 2...]
    psum x1 -> x0, blocking collectives: 42.8 us -> none  [on_device(): commands = lax.psum(partial_commands, 'layer')]
  transfers between devices with their start and end apart: 3 -> 0, of which waited for: 3 -> 0; matrix products, arithmetic and copies ran while one was open for 0% -> 0% of each run, Pallas kernels for 0% -> 0%
where the time goes in v2:
time: 49.7 us; the launch traced here: 49 us
  Pallas kernels  44.5 us (90%)
  local copies, waits for them, and re-layouts  2.5 us (5%)
  other arithmetic  1.3 us (3%)
  between operations  0.64 us (1%)
    pallas_call x1, Pallas kernels, on_device(): pl.pallas_call(frame_kernel, out_shape=(jax.ShapeDtypeStruct((1, STARS, 2...  44.5 us
    unnamed x2, local copies, waits for them, and re-layouts  2.5 us
    concatenate x1, other arithmetic, on_device(): jnp.concatenate([wind_shift.T, cone_offset], axis=0)  1.3 us

profile of v2, /device:TPU:1, one launch (start us, length us, event | category | flops | bytes accessed | tf_op | source)
XLA Modules:
  0.0 49.0 jit_solution(10590523818054222010)
XLA Ops:
  0.6 1.3 %pad_add_fusion.whole_ref = s32[8,32]{1,0:T(8,128)} fusion(s32[6,32]{1,0:T(8,128)} %param.8, s32[2,32]{1,0:T(2,128)} %bitcast.10), kind=kLoop, calls=%fused_computation | loop fusion | flops 256 | bytes 2048 | tf_op jit(solution)/shard_map/concatenate | solution.py:516
  1.9 44.5 %frame.1 = (f32[1,6,2,10]{3,2,1,0:T(2,128)}, f32[1,256]{1,0:T(1,128)}) custom-call(s32[8,32]{1,0:T(8,128)} %pad_add_fusion.whole_ref, f32[6,32]{1,0:T(8,128)} %cone_weight.1, s32[1,10]{1,0:T(1,128)} %lit_ref_in.1, f32[64,2048]{1,0:T(8,128)} %bitcast.9, bf16[15360,128]{1,0:T(8,128)(2,1)} %bitcast.8), custom_call_target="tpu_custom_call" | custom-call | tf_op jit(solution)/shard_map/frame/pallas_call | solution.py:467
  46.5 1.3 %copy.11 = f32[1,6,2,10]{3,2,1,0:T(2,128)} copy(f32[1,6,2,10]{3,2,1,0:T(2,128)} %get-tuple-element.8) | data formatting | bytes 960
  47.8 1.2 %copy.12 = f32[256]{0:T(256)} copy(f32[256]{0:T(256)} %bitcast.11) | data formatting | bytes 2048

commit v3 on v2

--- a/solution.py
+++ b/solution.py
@@ -65,17 +65,23 @@
 
 
 def frame_kernel(
-    whole_ref,
-    cone_weight,
-    lit_ref_in,
+    wind_hbm,
+    offset_hbm,
+    weight_hbm,
+    mask_hbm,
     screens_hbm,
     matrix_hbm,
     slopes_ref,
     commands_ref,
+    wind,
+    cone_offset,
+    cone_weight,
+    mask_ref,
     held,
     placed,
     partial,
     swapped,
+    crossed,
     coded,
     landed,
     filters,
@@ -92,6 +98,8 @@
     load_sem,
     swap_send,
     swap_recv,
+    cross_send,
+    cross_recv,
     code_send,
     code_recv,
     plane_send,
@@ -113,12 +121,18 @@
         return (tile_index, layer_index)
 
     partner = at(tile, layer + 1 - 2 * core)
-
-    def code_target(band, d):
-        return at((tile + band - 1 + TILES) % TILES, core * 4 + d)
-
-    def code_source(band, y):
-        return at((tile - (band - 1) + TILES) % TILES, y * 2 + half)
+    side = tile % 2
+    near_tile = tile + 1 - 2 * side
+    near_band = 2 - 2 * side
+    far_band = 2 * side
+    onward = at((tile + 4 * side - 2 + TILES) % TILES, layer)
+    backward = at((tile - 4 * side + 2 + TILES) % TILES, layer)
+
+    def code_target(near, d):
+        return at(near_tile if near else tile, core * 4 + d)
+
+    def code_source(near, y):
+        return at(near_tile if near else tile, y * 2 + half)
 
     def plane_peer(step):
         return at(along * 8 + (in_plane + step + 8) % 8, layer)
@@ -130,39 +144,62 @@
         return at(tile, (layer + step + 8) % 8)
 
     barrier = pltpu.get_barrier_semaphore()
+    loads = [
+        pltpu.make_async_copy(source, target, load_sem.at[k])
+        for k, (source, target) in enumerate(
+            (
+                (screens_hbm, held),
+                (wind_hbm, wind),
+                (offset_hbm, cone_offset),
+                (weight_hbm, cone_weight),
+                (mask_hbm, mask_ref),
+                (matrix_hbm, matrix),
+            )
+        )
+    ]
+    for load in loads:
+        load.start()
 
     def greet(where):
         pl.semaphore_signal(barrier, inc=1, device_id=where, device_id_type=MESH)
 
     greet(partner)
+    greet(backward)
     own_is_target = half == core
-    for band in range(3):
-        for y in range(4):
-            if band == 1:
-                @pl.when(jnp.logical_not(own_is_target & (chip_y == y)))
-                def _(band=band, y=y):
-                    greet(code_source(band, y))
-            else:
-                greet(code_source(band, y))
+    for y in range(4):
+        greet(code_source(True, y))
+
+        @pl.when(jnp.logical_not(own_is_target & (chip_y == y)))
+        def _(y=y):
+            greet(code_source(False, y))
+
     for step in range(1, 8):
         greet(plane_peer(-step))
         greet(line_peer(-step))
         greet(layer_peer(-step))
 
-    screens_load = pltpu.make_async_copy(screens_hbm, held, load_sem.at[0])
-    screens_load.start()
-    matrix_load = pltpu.make_async_copy(matrix_hbm, matrix, load_sem.at[1])
-    matrix_load.start()
-
-    zeros = jnp.zeros((32, 128), F32)
-    screens_load.wait()
+    zeros = jnp.zeros((5, 8, 128), F32)
+
+    def clear(k, carry):
+        placed[pl.ds(11 * k, 5)] = zeros
+        placed[pl.ds(11 * k + 8, 3)] = zeros[0:3]
+        return carry
+
+    lax.fori_loop(0, 64, clear, 0, unroll=8)
+    for load in loads[:4]:
+        load.wait()
+    row = iota((8, 128), 0)
     for slot in range(4):
-        down = whole_ref[0, layer * 4 + slot] + 16
+        down = (wind[0, layer * 4 + slot] + 16) & 7
+        early = row < down
         for m in range(16):
-            rows = held[16 * slot : 16 * slot + 16, 128 * m : 128 * m + 128]
-            placed[16 * slot + m] = pltpu.roll(
-                jnp.concatenate([rows, zeros], axis=0), down, axis=0
-            )
+            columns = slice(128 * m, 128 * m + 128)
+            upper = pltpu.roll(held[16 * slot : 16 * slot + 8, columns], down, axis=0)
+            lower = pltpu.roll(held[16 * slot + 8 : 16 * slot + 16, columns], down, axis=0)
+            group = 11 * (16 * slot + m) + 5
+            placed[group] = jnp.where(early, 0.0, upper)
+            placed[group + 1] = jnp.where(early, upper, lower)
+            placed[group + 2] = jnp.where(early, lower, 0.0)
 
     lane = iota((48, 128), 1)
 
@@ -172,21 +209,25 @@
             total = [None] * 5
             for slot in range(4):
                 which = layer * 4 + slot
-                beginning = whole_ref[1, which] + whole_ref[2 + star, which]
+                beginning = wind[1, which] + cone_offset[star, which]
                 weight = cone_weight[star, which]
-                first = lax.shift_right_logical(beginning, 7) + 5 * which_half + 16 * slot
+                column = lax.shift_right_logical(beginning, 7) + 5 * which_half + 16 * slot
+                first = 11 * column + 5 - lax.shift_right_logical(wind[0, which] + 16, 3)
                 turn = beginning & 127
                 roll_by = (128 - turn) & 127
                 stay = lane < 128 - turn
-                before = pltpu.roll(placed[first], roll_by, axis=1)
+
+                def turned(m, first=first, roll_by=roll_by):
+                    window = placed[pl.ds(first + 11 * m, 6)].reshape(48, 128)
+                    return pltpu.roll(window, roll_by, axis=1)
+
+                before = turned(0)
                 for m in range(5):
-                    after = pltpu.roll(placed[first + m + 1], roll_by, axis=1)
+                    after = turned(m + 1)
                     term = weight * jnp.where(stay, before, after)
                     total[m] = term if slot == 0 else total[m] + term
                     before = after
-            code = [
-                modulo_16(jnp.round(part * (1.0 / UNIT)).astype(jnp.int32)) for part in total
-            ]
+            code = [jnp.round(part * (1.0 / UNIT)).astype(jnp.int32) for part in total]
             for d in range(4):
                 start = 32 * d
                 main = code[d]
@@ -233,49 +274,63 @@
             partner,
         )
 
-    def code_copy(band, d):
-        return remote(
-            coded.at[band, d],
-            landed.at[band, chip_y],
-            code_send.at[band, d],
-            code_recv.at[band, chip_y],
-            code_target(band, d),
-        )
-
-    def code_arrival(band, y):
-        return remote(
-            coded.at[band, 0],
-            landed.at[band, y],
-            code_send.at[band, 0],
-            code_recv.at[band, y],
-            code_source(band, y),
+    def cross(d):
+        return remote(
+            coded.at[far_band, d], crossed.at[d], cross_send.at[d], cross_recv.at[d], onward
+        )
+
+    def code_copy(near, d):
+        return remote(
+            coded.at[near_band if near else 1, d],
+            landed.at[near, chip_y],
+            code_send.at[near, d],
+            code_recv.at[near, chip_y],
+            code_target(near, d),
+        )
+
+    def code_arrival(near, y):
+        return remote(
+            coded.at[near_band if near else 1, 0],
+            landed.at[near, y],
+            code_send.at[near, 0],
+            code_recv.at[near, y],
+            code_source(near, y),
         )
 
     add_layers(1 - core)
-    pl.semaphore_wait(barrier, 34 - own_is_target.astype(jnp.int32))
-    for band in range(3):
+    pl.semaphore_wait(barrier, 31 - own_is_target.astype(jnp.int32))
+    for band in (far_band, 1, near_band):
         swap(band).start()
     add_layers(core)
 
-    for band in range(3):
-        swap(band).wait_recv()
-        for d in range(4):
-            own = partial[band, core * 4 + d].astype(jnp.int32)
-            both = own + swapped[band, d].astype(jnp.int32)
-            coded[band, d] = modulo_16(both).astype(jnp.int16)
-        for d in range(4):
-            if band == 1:
-                is_self = core * 4 + d == layer
-
-                @pl.when(jnp.logical_not(is_self))
-                def _(band=band, d=d):
-                    code_copy(band, d).start()
-
-                @pl.when(is_self)
-                def _(band=band, d=d):
-                    landed[band, chip_y] = coded[band, d]
-            else:
-                code_copy(band, d).start()
+    def both(band, d):
+        own = partial[band, core * 4 + d].astype(jnp.int32)
+        return own + swapped[band, d].astype(jnp.int32)
+
+    swap(far_band).wait_recv()
+    for d in range(4):
+        coded[far_band, d] = both(far_band, d).astype(jnp.int16)
+        cross(d).start()
+    swap(1).wait_recv()
+    for d in range(4):
+        coded[1, d] = both(1, d).astype(jnp.int16)
+    for d in range(4):
+        is_self = core * 4 + d == layer
+
+        @pl.when(jnp.logical_not(is_self))
+        def _(d=d):
+            code_copy(0, d).start()
+
+        @pl.when(is_self)
+        def _(d=d):
+            landed[0, chip_y] = coded[1, d]
+
+    swap(near_band).wait_recv()
+    for d in range(4):
+        cross(d).wait_recv()
+        total = both(near_band, d) + crossed[d].astype(jnp.int32)
+        coded[near_band, d] = total.astype(jnp.int16)
+        code_copy(1, d).start()
 
     flips, odd = filter_tables()
     odd_high, odd_low = split(odd)
@@ -288,29 +343,29 @@
     wanted = jnp.where(source < 128, source >> 4, 8 + ((source >> 4) & 1))
     pick_ref[...] = jnp.where(wanted == column, 1.0 / 8192.0, 0.0).astype(BF16)
     spread = jnp.where(iota((10, 384), 0) == column[0:10], 1.0, 0.0)
-    lit_ref[...] = dot(lit_ref_in[...].astype(F32), spread)
-    place = iota((64, 1536), 1)
-    begin = 24 * iota((64, 1536), 0)
-    expand[...] = jnp.where((place >= begin) & (place < begin + 24), 1.0, 0.0).astype(BF16)
-    place = iota((16, 1536), 1)
+    loads[4].wait()
+    lit_ref[...] = dot(mask_ref[...].astype(F32), spread)
+    place = iota((8, 192), 1)
+    begin = 24 * iota((8, 192), 0)
+    expand[...] = jnp.where((place >= begin) & (place < begin + 24), 1.0, 0.0)
+    place = iota((16, 192), 1)
     entry = ((place >> 2) % 6) * 2 + (place & 1)
     for h in range(2):
-        wanted = (entry == iota((16, 1536), 0)) & (((place >> 1) & 1) == h)
+        wanted = (entry == iota((16, 192), 0)) & (((place >> 1) & 1) == h)
         keep[h] = jnp.where(wanted, 1.0, 0.0)
-
-    for band in range(3):
-        for y in range(4):
-            if band == 1:
-                @pl.when(jnp.logical_not(own_is_target & (chip_y == y)))
-                def _(band=band, y=y):
-                    code_arrival(band, y).wait_recv()
-            else:
-                code_arrival(band, y).wait_recv()
+    loads[5].wait()
 
     code = jnp.zeros((128, 128), jnp.int32)
-    for band in range(3):
-        for y in range(4):
-            code = code + landed[band, y].astype(jnp.int32)
+    for y in range(4):
+        @pl.when(jnp.logical_not(own_is_target & (chip_y == y)))
+        def _(y=y):
+            code_arrival(0, y).wait_recv()
+
+    for y in range(4):
+        code = code + landed[0, y].astype(jnp.int32)
+    for y in range(4):
+        code_arrival(1, y).wait_recv()
+        code = code + landed[1, y].astype(jnp.int32)
     code = modulo_16(code)
     field_imag = sine(code)
     field_real = sine(modulo_16(code + 16384))
@@ -401,22 +456,23 @@
     for step in range(1, 8):
         line_copy(step).start()
     line[along] = plane[...]
-    for step in range(1, 8):
-        line_arrival(step).wait_recv()
-
-    matrix_load.wait()
-    gathered = line[...].reshape(TILES, 256).astype(BF16)
-    rows = lax.dot_general(
-        gathered[:, 0:160],
-        expand[...],
-        (((0,), (0,)), ((), ())),
-        preferred_element_type=F32,
-    )
+
     total = jnp.zeros((32, 128), F32)
-    for j in range(10):
-        block = rows[16 * j : 16 * j + 16]
-        vector = jnp.concatenate([block * keep[0], block * keep[1]], axis=0).astype(BF16)
-        total = total + dot(vector, matrix[1536 * j : 1536 * j + 1536, :])
+    for step in (0, 1, 7, 2, 6, 3, 5, 4):
+        other = (along - step + 8) % 8
+        if step:
+            line_arrival(step).wait_recv()
+        rows = lax.dot_general(
+            line[other].reshape(8, 256)[:, 0:160],
+            expand[...],
+            (((0,), (0,)), ((), ())),
+            preferred_element_type=F32,
+        )
+        for j in range(10):
+            block = rows[16 * j : 16 * j + 16]
+            vector = jnp.concatenate([block * keep[0], block * keep[1]], axis=0).astype(BF16)
+            start = pl.multiple_of(1536 * j + 192 * other, 64)
+            total = total + dot(vector, matrix[pl.ds(start, 192), :])
     own_part[...] = jnp.concatenate(
         [
             jnp.sum(total[0:16], axis=0, keepdims=True),
@@ -439,25 +495,26 @@
     for step in range(1, 8):
         part_copy(step).start()
     parts[layer] = own_part[...]
+    for band in range(3):
+        swap(band).wait_send()
+    for d in range(4):
+        cross(d).wait_send()
+        code_copy(1, d).wait_send()
+
+        @pl.when(jnp.logical_not(core * 4 + d == layer))
+        def _(d=d):
+            code_copy(0, d).wait_send()
+
+    for step in range(1, 8):
+        plane_copy(step).wait_send()
+        line_copy(step).wait_send()
     for step in range(1, 8):
         part_arrival(step).wait_recv()
     total = parts[0]
     for k in range(1, 8):
         total = total + parts[k]
     commands_ref[...] = total
-
-    for band in range(3):
-        swap(band).wait_send()
-        for d in range(4):
-            if band == 1:
-                @pl.when(jnp.logical_not(core * 4 + d == layer))
-                def _(band=band, d=d):
-                    code_copy(band, d).wait_send()
-            else:
-                code_copy(band, d).wait_send()
-    for step in range(1, 8):
-        plane_copy(step).wait_send()
-        line_copy(step).wait_send()
+    for step in range(1, 8):
         part_copy(step).wait_send()
 
 
@@ -470,37 +527,38 @@
             jax.ShapeDtypeStruct((1, STARS, 2, 10), F32),
             jax.ShapeDtypeStruct((1, 256), F32),
         ),
-        in_specs=[
-            pl.BlockSpec(memory_space=pltpu.SMEM),
-            pl.BlockSpec(memory_space=pltpu.SMEM),
-            pl.BlockSpec(memory_space=pltpu.VMEM),
-            pl.BlockSpec(memory_space=pltpu.HBM),
-            pl.BlockSpec(memory_space=pltpu.HBM),
-        ],
+        in_specs=[pl.BlockSpec(memory_space=pltpu.HBM)] * 6,
         out_specs=[pl.BlockSpec(memory_space=pltpu.VMEM)] * 2,
         scratch_shapes=[
+            pltpu.SMEM((2, 32), jnp.int32),
+            pltpu.SMEM((STARS, 32), jnp.int32),
+            pltpu.SMEM((STARS, 32), F32),
+            pltpu.VMEM((1, 10), jnp.int32),
             pltpu.VMEM((64, 2048), F32),
-            pltpu.VMEM((64, 48, 128), F32),
+            pltpu.VMEM((64 * 11, 8, 128), F32),
             pltpu.VMEM((3, 8, 128, 128), jnp.int16),
             pltpu.VMEM((3, 4, 128, 128), jnp.int16),
+            pltpu.VMEM((4, 128, 128), jnp.int16),
             pltpu.VMEM((3, 4, 128, 128), jnp.int16),
-            pltpu.VMEM((3, 4, 128, 128), jnp.int16),
+            pltpu.VMEM((2, 4, 128, 128), jnp.int16),
             pltpu.VMEM((2, 128, 128), BF16),
             pltpu.VMEM((128, 128), BF16),
             pltpu.VMEM((256, 384), BF16),
             pltpu.VMEM((1, 384), F32),
-            pltpu.VMEM((64, 1536), BF16),
-            pltpu.VMEM((2, 16, 1536), F32),
+            pltpu.VMEM((8, 192), F32),
+            pltpu.VMEM((2, 16, 192), F32),
             pltpu.VMEM((8, 1, 256), F32),
             pltpu.VMEM((8, 8, 1, 256), F32),
             pltpu.VMEM((15360, 128), BF16),
             pltpu.VMEM((1, 256), F32),
             pltpu.VMEM((8, 1, 256), F32),
-            dma((2,)),
+            dma((6,)),
             dma((3,)),
             dma((3,)),
-            dma((3, 4)),
-            dma((3, 4)),
+            dma((4,)),
+            dma((4,)),
+            dma((2, 4)),
+            dma((2, 4)),
             dma((8,)),
             dma((8,)),
             dma((8,)),
@@ -513,7 +571,8 @@
         ),
         name="frame",
     )(
-        jnp.concatenate([wind_shift.T, cone_offset], axis=0),
+        wind_shift.T,
+        cone_offset,
         cone_weight,
         valid_mask,
         screens.reshape(64, 2048),

time: 49.7 us -> 46.3 us (0.932); the launches traced: 49 us -> 46.1 us
  Pallas kernels: 44.5 us -> 43 us
  other arithmetic: 1.3 us -> 0 us
    pallas_call x1, Pallas kernels: 44.5 us -> 43 us  [on_device(): pl.pallas_call(frame_kernel, out_shape=(jax.ShapeDtypeStruct((1, STARS, 2...]
    concatenate x1 -> x0, other arithmetic: 1.3 us -> none  [on_device(): jnp.concatenate([wind_shift.T, cone_offset], axis=0)]
where the time goes in v3:
time: 46.3 us; the launch traced here: 46.1 us
  Pallas kernels  43 us (93%)
  local copies, waits for them, and re-layouts  2.5 us (5%)
  between operations  0.64 us (1%)
    pallas_call x1, Pallas kernels, on_device(): pl.pallas_call(frame_kernel, out_shape=(jax.ShapeDtypeStruct((1, STARS, 2...  43 us
    unnamed x2, local copies, waits for them, and re-layouts  2.5 us

profile of v3, /device:TPU:1, one launch (start us, length us, event | category | flops | bytes accessed | tf_op | source)
XLA Modules:
  0.0 46.1 jit_solution(14073754166685752143)
XLA Ops:
  0.6 43.0 %frame.1 = (f32[1,6,2,10]{3,2,1,0:T(2,128)}, f32[1,256]{1,0:T(1,128)}) custom-call(s32[2,32]{1,0:T(2,128)} %bitcast.11, s32[6,32]{1,0:T(8,128)} %offset_hbm.1, f32[6,32]{1,0:T(8,128)} %weight_hbm.1, s32[1,10]{1,0:T(1,128)} %mask_hbm.1, f32[64,2048]{1,0:T(8,128)} %bitcast.9, bf16[15360,128]{1,0:T(8,128)(2,1)} %bitcast.8), custom_call_target="tpu_custom_call" | custom-call | tf_op jit(solution)/shard_map/frame/pallas_call | solution.py:524
  43.6 1.3 %copy.11 = f32[1,6,2,10]{3,2,1,0:T(2,128)} copy(f32[1,6,2,10]{3,2,1,0:T(2,128)} %get-tuple-element.8) | data formatting | bytes 960
  44.9 1.2 %copy.12 = f32[256]{0:T(256)} copy(f32[256]{0:T(256)} %bitcast.10) | data formatting | bytes 2048

commit v4 on v3

--- a/solution.py
+++ b/solution.py
@@ -201,59 +201,53 @@
             placed[group + 1] = jnp.where(early, upper, lower)
             placed[group + 2] = jnp.where(early, lower, 0.0)
 
-    lane = iota((48, 128), 1)
-
-    def add_layers(which_half):
-        tails = [None] * 4
+    lane = iota((16, 128), 1)
+
+    def add_layers(band):
+        tails = [None] * 8
         for star in range(STARS):
-            total = [None] * 5
+            total = [None] * 10
             for slot in range(4):
                 which = layer * 4 + slot
                 beginning = wind[1, which] + cone_offset[star, which]
                 weight = cone_weight[star, which]
-                column = lax.shift_right_logical(beginning, 7) + 5 * which_half + 16 * slot
+                column = lax.shift_right_logical(beginning, 7) + 16 * slot
                 first = 11 * column + 5 - lax.shift_right_logical(wind[0, which] + 16, 3)
+                first = first + 2 * band
                 turn = beginning & 127
                 roll_by = (128 - turn) & 127
                 stay = lane < 128 - turn
 
                 def turned(m, first=first, roll_by=roll_by):
-                    window = placed[pl.ds(first + 11 * m, 6)].reshape(48, 128)
+                    window = placed[pl.ds(first + 11 * m, 2)].reshape(16, 128)
                     return pltpu.roll(window, roll_by, axis=1)
 
                 before = turned(0)
-                for m in range(5):
+                for m in range(10):
                     after = turned(m + 1)
                     term = weight * jnp.where(stay, before, after)
                     total[m] = term if slot == 0 else total[m] + term
                     before = after
             code = [jnp.round(part * (1.0 / UNIT)).astype(jnp.int32) for part in total]
-            for d in range(4):
-                start = 32 * d
-                main = code[d]
-                if d > 0:
+            for block in range(8):
+                tile_at, start = (block * SPAN) // 128, (block * SPAN) % 128
+                main = code[tile_at]
+                if start > 0:
                     main = jnp.where(
                         lane < 128 - start,
-                        pltpu.roll(code[d], 128 - start, axis=1),
-                        pltpu.roll(code[d + 1], 128 - start, axis=1),
+                        pltpu.roll(main, 128 - start, axis=1),
+                        pltpu.roll(code[tile_at + 1], 128 - start, axis=1),
                     )
                 place = 32 * (star % 4)
-                tail = code[d + 1]
+                tail = code[tile_at + 1]
                 if place != start:
                     tail = pltpu.roll(tail, (place - start) % 128, axis=1)
                 tail = jnp.where((lane >= place) & (lane < place + 32), tail, 0)
-                tails[d] = tail if star % 4 == 0 else tails[d] + tail
-                for band in range(3):
-                    rows = slice(16 * band, 16 * band + 16)
-                    block = 4 * which_half + d
-                    partial[band, block, 16 * star : 16 * star + 16, :] = main[rows].astype(
-                        jnp.int16
-                    )
-                    if star in (3, 5):
-                        at_row = 96 + 16 * (star // 4)
-                        partial[band, block, at_row : at_row + 16, :] = tails[d][rows].astype(
-                            jnp.int16
-                        )
+                tails[block] = tail if star % 4 == 0 else tails[block] + tail
+                partial[band, block, 16 * star : 16 * star + 16, :] = main.astype(jnp.int16)
+                if star in (3, 5):
+                    at_row = 96 + 16 * (star // 4)
+                    partial[band, block, at_row : at_row + 16, :] = tails[block].astype(jnp.int16)
 
     def remote(source, target, send, recv, where):
         return pltpu.make_async_remote_copy(
@@ -297,20 +291,21 @@
             code_source(near, y),
         )
 
-    add_layers(1 - core)
-    pl.semaphore_wait(barrier, 31 - own_is_target.astype(jnp.int32))
-    for band in (far_band, 1, near_band):
-        swap(band).start()
-    add_layers(core)
-
     def both(band, d):
         own = partial[band, core * 4 + d].astype(jnp.int32)
         return own + swapped[band, d].astype(jnp.int32)
 
+    add_layers(far_band)
+    pl.semaphore_wait(barrier, 31 - own_is_target.astype(jnp.int32))
+    swap(far_band).start()
+    add_layers(1)
+    swap(1).start()
     swap(far_band).wait_recv()
     for d in range(4):
         coded[far_band, d] = both(far_band, d).astype(jnp.int16)
         cross(d).start()
+    add_layers(near_band)
+    swap(near_band).start()
     swap(1).wait_recv()
     for d in range(4):
         coded[1, d] = both(1, d).astype(jnp.int16)
@@ -516,6 +511,32 @@
     commands_ref[...] = total
     for step in range(1, 8):
         part_copy(step).wait_send()
+
+
+def publish_kernel(slopes_in, commands_in, slopes_ref, commands_ref, sem):
+    copies = [
+        pltpu.make_async_copy(slopes_in, slopes_ref, sem.at[0]),
+        pltpu.make_async_copy(commands_in, commands_ref, sem.at[1]),
+    ]
+    for copy in copies:
+        copy.start()
+    for copy in copies:
+        copy.wait()
+
+
+def publish(slopes, commands):
+    return pl.pallas_call(
+        publish_kernel,
+        out_shape=(
+            jax.ShapeDtypeStruct(slopes.shape, F32),
+            jax.ShapeDtypeStruct(commands.shape, F32),
+        ),
+        in_specs=[pl.BlockSpec(memory_space=pltpu.HBM)] * 2,
+        out_specs=[pl.BlockSpec(memory_space=pltpu.HBM)] * 2,
+        scratch_shapes=[pltpu.SemaphoreType.DMA((2,))],
+        compiler_params=pltpu.CompilerParams(vmem_limit_bytes=66_900_000),
+        name="publish",
+    )(slopes, commands)
 
 
 def on_device(screens, wind_shift, cone_offset, cone_weight, valid_mask, reconstructor):
@@ -578,6 +599,7 @@
         screens.reshape(64, 2048),
         matrix,
     )
+    slopes, commands = publish(slopes, commands)
     return slopes, commands.reshape(-1)
 
 

time: 46.3 us -> 45.1 us (0.974)
  local copies, waits for them, and re-layouts: 2.5 us -> 0 us
  Pallas kernels: 43 us -> 44.3 us
    unnamed x2 -> x0, local copies, waits for them, and re-layouts: 2.5 us -> none
    pallas_call x0 -> x1, Pallas kernels: none -> 1.34 us  [publish(): pl.pallas_call(publish_kernel, out_shape=(jax.ShapeDtypeStruct(slopes.sha...]
where the time goes in v4:
time: 45.1 us; the launch traced here: 44.9 us
  Pallas kernels  44.3 us (98%)
  between operations  0.64 us (1%)
    pallas_call x1, Pallas kernels, on_device(): pl.pallas_call(frame_kernel, out_shape=(jax.ShapeDtypeStruct((1, STARS, 2...  43 us
    pallas_call x1, Pallas kernels, publish(): pl.pallas_call(publish_kernel, out_shape=(jax.ShapeDtypeStruct(slopes.sha...  1.34 us

profile of v4, /device:TPU:1, one launch (start us, length us, event | category | flops | bytes accessed | tf_op | source)
XLA Modules:
  0.0 44.9 jit_solution(14554356442154055526)
XLA Ops:
  0.6 43.0 %frame.1 = (f32[1,6,2,10]{3,2,1,0:T(2,128)}, f32[1,256]{1,0:T(1,128)}) custom-call(s32[2,32]{1,0:T(2,128)} %bitcast.10, s32[6,32]{1,0:T(8,128)} %offset_hbm.1, f32[6,32]{1,0:T(8,128)} %weight_hbm.1, s32[1,10]{1,0:T(1,128)} %mask_hbm.1, f32[64,2048]{1,0:T(8,128)} %bitcast.9, bf16[15360,128]{1,0:T(8,128)(2,1)} %bitcast.8), custom_call_target="tpu_custom_call" | custom-call | tf_op jit(solution)/shard_map/frame/pallas_call | solution.py:545
  43.6 1.3 %publish.1 = (f32[1,6,2,10]{3,2,1,0:T(2,128)}, f32[1,256]{1,0:T(1,128)}) custom-call(f32[1,6,2,10]{3,2,1,0:T(2,128)} %get-tuple-element.6.slopes_in, f32[1,256]{1,0:T(1,128)} %get-tuple-element.7.commands_in), custom_call_target="tpu_custom_call" | custom-call | tf_op jit(solution)/shard_map/publish/pallas_call | solution.py:528

commit v5 on v4

--- a/solution.py
+++ b/solution.py
@@ -163,20 +163,16 @@
     def greet(where):
         pl.semaphore_signal(barrier, inc=1, device_id=where, device_id_type=MESH)
 
-    greet(partner)
-    greet(backward)
     own_is_target = half == core
+    for step in (4, 3, 5, 2, 6, 1, 7):
+        greet(layer_peer(step))
     for y in range(4):
         greet(code_source(True, y))
-
-        @pl.when(jnp.logical_not(own_is_target & (chip_y == y)))
-        def _(y=y):
-            greet(code_source(False, y))
-
-    for step in range(1, 8):
-        greet(plane_peer(-step))
-        greet(line_peer(-step))
-        greet(layer_peer(-step))
+    for step in (4, 3, 5, 2, 6, 1, 7):
+        greet(line_peer(step))
+    for step in range(1, 8):
+        greet(plane_peer(step))
+    greet(backward)
 
     zeros = jnp.zeros((5, 8, 128), F32)
 
@@ -296,16 +292,16 @@
         return own + swapped[band, d].astype(jnp.int32)
 
     add_layers(far_band)
-    pl.semaphore_wait(barrier, 31 - own_is_target.astype(jnp.int32))
+    add_layers(1)
+    pl.semaphore_wait(barrier, 26)
     swap(far_band).start()
-    add_layers(1)
     swap(1).start()
+    add_layers(near_band)
+    swap(near_band).start()
     swap(far_band).wait_recv()
     for d in range(4):
         coded[far_band, d] = both(far_band, d).astype(jnp.int16)
         cross(d).start()
-    add_layers(near_band)
-    swap(near_band).start()
     swap(1).wait_recv()
     for d in range(4):
         coded[1, d] = both(1, d).astype(jnp.int16)
@@ -453,10 +449,11 @@
     line[along] = plane[...]
 
     total = jnp.zeros((32, 128), F32)
-    for step in (0, 1, 7, 2, 6, 3, 5, 4):
-        other = (along - step + 8) % 8
-        if step:
-            line_arrival(step).wait_recv()
+    for other in range(8):
+        @pl.when(along != other)
+        def _(other=other):
+            line_arrival((along - other + 8) % 8).wait_recv()
+
         rows = lax.dot_general(
             line[other].reshape(8, 256)[:, 0:160],
             expand[...],
@@ -466,8 +463,8 @@
         for j in range(10):
             block = rows[16 * j : 16 * j + 16]
             vector = jnp.concatenate([block * keep[0], block * keep[1]], axis=0).astype(BF16)
-            start = pl.multiple_of(1536 * j + 192 * other, 64)
-            total = total + dot(vector, matrix[pl.ds(start, 192), :])
+            start = 1536 * j + 192 * other
+            total = total + dot(vector, matrix[start : start + 192, :])
     own_part[...] = jnp.concatenate(
         [
             jnp.sum(total[0:16], axis=0, keepdims=True),

time: 45.1 us -> 44.1 us (0.978)
  Pallas kernels: 44.3 us -> 43.3 us
    pallas_call x1, Pallas kernels: 43 us -> 42 us  [on_device(): pl.pallas_call(frame_kernel, out_shape=(jax.ShapeDtypeStruct((1, STARS, 2...]
where the time goes in v5:
time: 44.1 us; the launch traced here: 43.9 us
  Pallas kernels  43.3 us (98%)
  between operations  0.64 us (1%)
    pallas_call x1, Pallas kernels, on_device(): pl.pallas_call(frame_kernel, out_shape=(jax.ShapeDtypeStruct((1, STARS, 2...  42 us
    pallas_call x1, Pallas kernels, publish(): pl.pallas_call(publish_kernel, out_shape=(jax.ShapeDtypeStruct(slopes.sha...  1.34 us

profile of v5, /device:TPU:1, one launch (start us, length us, event | category | flops | bytes accessed | tf_op | source)
XLA Modules:
  0.0 43.9 jit_solution(10433907626289223039)
XLA Ops:
  0.6 42.0 %frame.1 = (f32[1,6,2,10]{3,2,1,0:T(2,128)}, f32[1,256]{1,0:T(1,128)}) custom-call(s32[2,32]{1,0:T(2,128)} %bitcast.10, s32[6,32]{1,0:T(8,128)} %offset_hbm.1, f32[6,32]{1,0:T(8,128)} %weight_hbm.1, s32[1,10]{1,0:T(1,128)} %mask_hbm.1, f32[64,2048]{1,0:T(8,128)} %bitcast.9, bf16[15360,128]{1,0:T(8,128)(2,1)} %bitcast.8), custom_call_target="tpu_custom_call" | custom-call | tf_op jit(solution)/shard_map/frame/pallas_call | solution.py:542
  42.6 1.3 %publish.1 = (f32[1,6,2,10]{3,2,1,0:T(2,128)}, f32[1,256]{1,0:T(1,128)}) custom-call(f32[1,6,2,10]{3,2,1,0:T(2,128)} %get-tuple-element.6.slopes_in, f32[1,256]{1,0:T(1,128)} %get-tuple-element.7.commands_in), custom_call_target="tpu_custom_call" | custom-call | tf_op jit(solution)/shard_map/publish/pallas_call | solution.py:525

commit v6 on v5

--- a/solution.py
+++ b/solution.py
@@ -71,8 +71,9 @@
     mask_hbm,
     screens_hbm,
     matrix_hbm,
+    slopes_hbm,
+    parts,
     slopes_ref,
-    commands_ref,
     wind,
     cone_offset,
     cone_weight,
@@ -90,22 +91,19 @@
     lit_ref,
     expand,
     keep,
-    plane,
-    line,
+    gathered,
     matrix,
     own_part,
-    parts,
     load_sem,
+    result_sem,
     swap_send,
     swap_recv,
     cross_send,
     cross_recv,
     code_send,
     code_recv,
-    plane_send,
-    plane_recv,
-    line_send,
-    line_recv,
+    row_send,
+    row_recv,
     part_send,
     part_recv,
 ):
@@ -114,7 +112,6 @@
     chip_y = layer // 2
     core = layer % 2
     half = layer // 4
-    in_plane = tile % 8
     along = tile // 8
 
     def at(tile_index, layer_index):
@@ -134,11 +131,8 @@
     def code_source(near, y):
         return at(near_tile if near else tile, y * 2 + half)
 
-    def plane_peer(step):
-        return at(along * 8 + (in_plane + step + 8) % 8, layer)
-
-    def line_peer(step):
-        return at(((along + step + 8) % 8) * 8 + in_plane, layer)
+    def tile_peer(step):
+        return at((tile + step) % TILES, layer)
 
     def layer_peer(step):
         return at(tile, (layer + step + 8) % 8)
@@ -148,16 +142,19 @@
         pltpu.make_async_copy(source, target, load_sem.at[k])
         for k, (source, target) in enumerate(
             (
-                (screens_hbm, held),
                 (wind_hbm, wind),
                 (offset_hbm, cone_offset),
                 (weight_hbm, cone_weight),
+                (screens_hbm.at[0:16], held.at[0:16]),
+                (screens_hbm.at[16:32], held.at[16:32]),
+                (screens_hbm.at[32:48], held.at[32:48]),
+                (screens_hbm.at[48:64], held.at[48:64]),
                 (mask_hbm, mask_ref),
                 (matrix_hbm, matrix),
             )
         )
     ]
-    for load in loads:
+    for load in loads[:8]:
         load.start()
 
     def greet(where):
@@ -168,11 +165,13 @@
         greet(layer_peer(step))
     for y in range(4):
         greet(code_source(True, y))
-    for step in (4, 3, 5, 2, 6, 1, 7):
-        greet(line_peer(step))
-    for step in range(1, 8):
-        greet(plane_peer(step))
     greet(backward)
+
+    def greet_tile(step, carry):
+        greet(tile_peer(step))
+        return carry
+
+    lax.fori_loop(1, TILES, greet_tile, 0)
 
     zeros = jnp.zeros((5, 8, 128), F32)
 
@@ -182,10 +181,11 @@
         return carry
 
     lax.fori_loop(0, 64, clear, 0, unroll=8)
-    for load in loads[:4]:
+    for load in loads[:3]:
         load.wait()
     row = iota((8, 128), 0)
     for slot in range(4):
+        loads[3 + slot].wait()
         down = (wind[0, layer * 4 + slot] + 16) & 7
         early = row < down
         for m in range(16):
@@ -197,6 +197,7 @@
             placed[group + 1] = jnp.where(early, upper, lower)
             placed[group + 2] = jnp.where(early, lower, 0.0)
 
+    loads[8].start()
     lane = iota((16, 128), 1)
 
     def add_layers(band):
@@ -293,7 +294,7 @@
 
     add_layers(far_band)
     add_layers(1)
-    pl.semaphore_wait(barrier, 26)
+    pl.semaphore_wait(barrier, 12 + TILES - 1)
     swap(far_band).start()
     swap(1).start()
     add_layers(near_band)
@@ -334,7 +335,7 @@
     wanted = jnp.where(source < 128, source >> 4, 8 + ((source >> 4) & 1))
     pick_ref[...] = jnp.where(wanted == column, 1.0 / 8192.0, 0.0).astype(BF16)
     spread = jnp.where(iota((10, 384), 0) == column[0:10], 1.0, 0.0)
-    loads[4].wait()
+    loads[7].wait()
     lit_ref[...] = dot(mask_ref[...].astype(F32), spread)
     place = iota((8, 192), 1)
     begin = 24 * iota((8, 192), 0)
@@ -344,7 +345,7 @@
     for h in range(2):
         wanted = (entry == iota((16, 192), 0)) & (((place >> 1) & 1) == h)
         keep[h] = jnp.where(wanted, 1.0, 0.0)
-    loads[5].wait()
+    loads[8].wait()
 
     code = jnp.zeros((128, 128), jnp.int32)
     for y in range(4):
@@ -402,60 +403,47 @@
     for star in range(STARS):
         for axis in range(2):
             slopes_ref[0, star, axis, :] = measured[axis * 8 + star, 0:10]
+    slopes_out = pltpu.make_async_copy(slopes_ref, slopes_hbm, result_sem.at[0])
+    slopes_out.start()
     lane_16 = iota((16, 256), 1)
     row_16 = iota((16, 256), 0)
     entry = (row_16 & 7) * 2 + (row_16 >> 3)
     coarse = measured[:, 128:384].astype(BF16).astype(F32)
     flat = jnp.where(((lane_16 & 15) == entry) & (entry < 12), coarse, 0.0)
-    plane[in_plane] = jnp.sum(flat, axis=0, keepdims=True)
-
-    def plane_copy(step):
+    gathered[tile] = jnp.sum(flat, axis=0, keepdims=True)
+
+    def row_copy(step):
         return remote(
-            plane.at[in_plane],
-            plane.at[in_plane],
-            plane_send.at[step],
-            plane_recv.at[step],
-            plane_peer(step),
-        )
-
-    def plane_arrival(step):
-        other = (in_plane - step + 8) % 8
-        return remote(
-            plane.at[in_plane],
-            plane.at[other],
-            plane_send.at[step],
-            plane_recv.at[step],
-            plane_peer(-step),
-        )
-
-    for step in range(1, 8):
-        plane_copy(step).start()
-    for step in range(1, 8):
-        plane_arrival(step).wait_recv()
-
-    def line_copy(step):
-        return remote(
-            plane, line.at[along], line_send.at[step], line_recv.at[step], line_peer(step)
-        )
-
-    def line_arrival(step):
-        other = (along - step + 8) % 8
-        return remote(
-            plane, line.at[other], line_send.at[step], line_recv.at[step], line_peer(-step)
-        )
-
-    for step in range(1, 8):
-        line_copy(step).start()
-    line[along] = plane[...]
+            gathered.at[tile],
+            gathered.at[tile],
+            row_send,
+            row_recv.at[along],
+            tile_peer(step),
+        )
+
+    def send_row(step, carry):
+        row_copy(step).start()
+        return carry
+
+    lax.fori_loop(8, TILES, send_row, 0)
+    lax.fori_loop(1, 8, send_row, 0)
+
+    def rows_wait(first, count, z):
+        rows = gathered.at[pl.ds(first, count)]
+        return remote(rows, rows, row_send, row_recv.at[z], tile_peer(1))
 
     total = jnp.zeros((32, 128), F32)
     for other in range(8):
         @pl.when(along != other)
         def _(other=other):
-            line_arrival((along - other + 8) % 8).wait_recv()
+            rows_wait(8 * other, 8, other).wait_recv()
+
+        @pl.when(along == other)
+        def _(other=other):
+            rows_wait(8 * other, 7, other).wait_recv()
 
         rows = lax.dot_general(
-            line[other].reshape(8, 256)[:, 0:160],
+            gathered[8 * other : 8 * other + 8].reshape(8, 256)[:, 0:160],
             expand[...],
             (((0,), (0,)), ((), ())),
             preferred_element_type=F32,
@@ -486,7 +474,8 @@
 
     for step in range(1, 8):
         part_copy(step).start()
-    parts[layer] = own_part[...]
+    part_out = pltpu.make_async_copy(own_part, parts.at[layer], result_sem.at[1])
+    part_out.start()
     for band in range(3):
         swap(band).wait_send()
     for d in range(4):
@@ -497,57 +486,63 @@
         def _(d=d):
             code_copy(0, d).wait_send()
 
-    for step in range(1, 8):
-        plane_copy(step).wait_send()
-        line_copy(step).wait_send()
+    rows_wait(0, TILES - 1, 0).wait_send()
+    slopes_out.wait()
+    part_out.wait()
     for step in range(1, 8):
         part_arrival(step).wait_recv()
-    total = parts[0]
-    for k in range(1, 8):
-        total = total + parts[k]
-    commands_ref[...] = total
     for step in range(1, 8):
         part_copy(step).wait_send()
 
 
-def publish_kernel(slopes_in, commands_in, slopes_ref, commands_ref, sem):
-    copies = [
-        pltpu.make_async_copy(slopes_in, slopes_ref, sem.at[0]),
-        pltpu.make_async_copy(commands_in, commands_ref, sem.at[1]),
-    ]
-    for copy in copies:
-        copy.start()
-    for copy in copies:
-        copy.wait()
-
-
-def publish(slopes, commands):
+def publish_kernel(slopes_in, parts_in, slopes_ref, commands_ref, parts, total, sem):
+    slopes_copy = pltpu.make_async_copy(slopes_in, slopes_ref, sem.at[0])
+    slopes_copy.start()
+    load = pltpu.make_async_copy(parts_in, parts, sem.at[1])
+    load.start()
+    load.wait()
+    added = parts[0]
+    for k in range(1, 8):
+        added = added + parts[k]
+    total[...] = added
+    store = pltpu.make_async_copy(total, commands_ref, sem.at[2])
+    store.start()
+    store.wait()
+    slopes_copy.wait()
+
+
+def publish(slopes, parts):
     return pl.pallas_call(
         publish_kernel,
         out_shape=(
             jax.ShapeDtypeStruct(slopes.shape, F32),
-            jax.ShapeDtypeStruct(commands.shape, F32),
+            jax.ShapeDtypeStruct((1, 256), F32),
         ),
         in_specs=[pl.BlockSpec(memory_space=pltpu.HBM)] * 2,
         out_specs=[pl.BlockSpec(memory_space=pltpu.HBM)] * 2,
-        scratch_shapes=[pltpu.SemaphoreType.DMA((2,))],
+        scratch_shapes=[
+            pltpu.VMEM((8, 1, 256), F32),
+            pltpu.VMEM((1, 256), F32),
+            pltpu.SemaphoreType.DMA((3,)),
+        ],
         compiler_params=pltpu.CompilerParams(vmem_limit_bytes=66_900_000),
         name="publish",
-    )(slopes, commands)
+    )(slopes, parts)
 
 
 def on_device(screens, wind_shift, cone_offset, cone_weight, valid_mask, reconstructor):
     dma = pltpu.SemaphoreType.DMA
     matrix = reconstructor.reshape(3840, 2, 2, 128).transpose(0, 2, 1, 3).reshape(15360, 128)
-    slopes, commands = pl.pallas_call(
+    slopes, parts = pl.pallas_call(
         frame_kernel,
         out_shape=(
             jax.ShapeDtypeStruct((1, STARS, 2, 10), F32),
-            jax.ShapeDtypeStruct((1, 256), F32),
+            jax.ShapeDtypeStruct((8, 1, 256), F32),
         ),
         in_specs=[pl.BlockSpec(memory_space=pltpu.HBM)] * 6,
-        out_specs=[pl.BlockSpec(memory_space=pltpu.VMEM)] * 2,
+        out_specs=[pl.BlockSpec(memory_space=pltpu.HBM)] * 2,
         scratch_shapes=[
+            pltpu.VMEM((1, STARS, 2, 10), F32),
             pltpu.SMEM((2, 32), jnp.int32),
             pltpu.SMEM((STARS, 32), jnp.int32),
             pltpu.SMEM((STARS, 32), F32),
@@ -565,21 +560,18 @@
             pltpu.VMEM((1, 384), F32),
             pltpu.VMEM((8, 192), F32),
             pltpu.VMEM((2, 16, 192), F32),
-            pltpu.VMEM((8, 1, 256), F32),
-            pltpu.VMEM((8, 8, 1, 256), F32),
+            pltpu.VMEM((TILES, 1, 256), F32),
             pltpu.VMEM((15360, 128), BF16),
             pltpu.VMEM((1, 256), F32),
-            pltpu.VMEM((8, 1, 256), F32),
-            dma((6,)),
+            dma((9,)),
+            dma((2,)),
             dma((3,)),
             dma((3,)),
             dma((4,)),
             dma((4,)),
             dma((2, 4)),
             dma((2, 4)),
-            dma((8,)),
-            dma((8,)),
-            dma((8,)),
+            dma,
             dma((8,)),
             dma((8,)),
             dma((8,)),
@@ -596,7 +588,7 @@
         screens.reshape(64, 2048),
         matrix,
     )
-    slopes, commands = publish(slopes, commands)
+    slopes, commands = publish(slopes, parts)
     return slopes, commands.reshape(-1)
 
 

time: 44.1 us -> 43.7 us (level)
  Pallas kernels: 43.3 us -> 42.8 us
    pallas_call x1, Pallas kernels: 42 us -> 41.5 us  [on_device(): pl.pallas_call(frame_kernel, out_shape=(jax.ShapeDtypeStruct((1, STARS, 2...]
where the time goes in v6:
time: 43.7 us; the launch traced here: 43.5 us
  Pallas kernels  42.8 us (98%)
  between operations  0.64 us (1%)
    pallas_call x1, Pallas kernels, on_device(): pl.pallas_call(frame_kernel, out_shape=(jax.ShapeDtypeStruct((1, STARS, 2...  41.5 us
    pallas_call x1, Pallas kernels, publish(): pl.pallas_call(publish_kernel, out_shape=(jax.ShapeDtypeStruct(slopes.sha...  1.32 us

profile of v6, /device:TPU:1, one launch (start us, length us, event | category | flops | bytes accessed | tf_op | source)
XLA Modules:
  0.0 43.5 jit_solution(2278791524680803615)
XLA Ops:
  0.6 41.5 %frame.1 = (f32[1,6,2,10]{3,2,1,0:T(2,128)}, f32[8,1,256]{2,1,0:T(1,128)}) custom-call(s32[2,32]{1,0:T(2,128)} %bitcast.10, s32[6,32]{1,0:T(8,128)} %offset_hbm.1, f32[6,32]{1,0:T(8,128)} %weight_hbm.1, s32[1,10]{1,0:T(1,128)} %mask_hbm.1, f32[64,2048]{1,0:T(8,128)} %bitcast.9, bf16[15360,128]{1,0:T(8,128)(2,1)} %bitcast.8), custom_call_target="tpu_custom_call" | custom-call | tf_op jit(solution)/shard_map/frame/pallas_call | solution.py:536
  42.2 1.3 %publish.1 = (f32[1,6,2,10]{3,2,1,0:T(2,128)}, f32[1,256]{1,0:T(1,128)}) custom-call(f32[1,6,2,10]{3,2,1,0:T(2,128)} %get-tuple-element.6.slopes_in, f32[8,1,256]{2,1,0:T(1,128)} %get-tuple-element.7.parts_in), custom_call_target="tpu_custom_call" | custom-call | tf_op jit(solution)/shard_map/publish/pallas_call | solution.py:515
